TPU v7x, 32 devices: a whole 2x2x4 slice. The times are simulated.
32 devices in a mesh: member: 4 (over x, core), tile: 8 (over z, y).
Axes of the slice: x: 2, y: 2, z: 4, core: 2. Of those that a mesh axis runs over, the one named last changes fastest.
Arguments:
- fields: float32 [8, 48, 3072], P('member', 'tile'), may hold values from 0 to 15, as said below
Outputs:
- frequencies: float32 [26, 48, 3072], P(None, 'tile', 'member')
Inputs may be any that keep to these rules, and one draw needn't show every extreme that they name: `fields`: every entry is a whole number.
All inputs are finite; a program needn't handle non-finite values.
Results may differ from a plain program's by a relative error of at most 0.0003.
Values may be sent and summed in bfloat16 or wider, within the bound.
No kernel may reach another device: no remote copies, remote signals or barrier semaphores. Data moves between devices by JAX's collectives and lax.ppermute only.
A program may use at most 64 MiB of HBM per device.

v0:
```python
import jax
import jax.numpy as jnp
from jax import lax
from jax.sharding import PartitionSpec as P

NZ = 192


barrier_level = 1000000.0
offset_table = [
    (a, b, c) for a in (-1, 0, 1) for b in (-1, 0, 1) for c in (-1, 0, 1) if (a, b, c) != (0, 0, 0)
]


def with_halo(shard, sides, width):
    for axis, dim in sides:
        devices, length = (lax.axis_size(axis), shard.shape[dim])
        up = [(i, (i + 1) % devices) for i in range(devices - 1)]
        down = [(j, i) for i, j in up]
        last = lax.slice_in_dim(shard, length - width, length, axis=dim)
        leading = lax.slice_in_dim(shard, 0, width, axis=dim)
        before = lax.ppermute(last, axis, up)
        after = lax.ppermute(leading, axis, down)
        shard = jnp.concatenate([before, shard, after], axis=dim)
    return shard


def direction_counts(padded):
    planes = padded.shape[1] - 2
    rows_here = padded.shape[2] - 2
    depth = padded.shape[3] - 2
    center = padded[:, 1 : planes + 1, 1 : rows_here + 1, 1 : depth + 1]
    descents = []
    for offset in offset_table:
        moved = padded[
            :,
            1 + offset[0] : 1 + offset[0] + planes,
            1 + offset[1] : 1 + offset[1] + rows_here,
            1 + offset[2] : 1 + offset[2] + depth,
        ]
        descents.append(moved - center)
    deepest = jnp.zeros_like(center)
    for drop in descents:
        deepest = jnp.minimum(deepest, drop)
    claimed = jnp.zeros(center.shape, bool)
    tallies = []
    for drop in descents:
        chosen = (drop == deepest) & (deepest < 0) & jnp.logical_not(claimed)
        tallies.append(jnp.sum(chosen.astype(jnp.float32), axis=0))
        claimed = claimed | chosen
    return jnp.stack(tallies)


def seal_edges(padded, axis_dim, position, extent):
    layer = lax.broadcasted_iota(jnp.int32, padded.shape, axis_dim)
    last = padded.shape[axis_dim] - 1
    outside = (layer == 0) & (position == 0) | (layer == last) & (position == extent - 1)
    return jnp.where(outside, barrier_level, padded)


def local(fields):
    tile_count = lax.axis_size("tile")
    member_count = lax.axis_size("member")
    total_members = fields.shape[0] * member_count
    row_count = fields.shape[2] // NZ
    shaped = fields.reshape(fields.shape[0], fields.shape[1], row_count, NZ)
    extended = with_halo(shaped.astype(jnp.bfloat16), (("tile", 1),), 1).astype(shaped.dtype)
    extended = seal_edges(extended, 1, lax.axis_index("tile"), tile_count)
    padded = jnp.pad(extended, ((0, 0), (0, 0), (1, 1), (1, 1)), constant_values=barrier_level)
    tallies = direction_counts(padded)
    flat_tallies = tallies.reshape(tallies.shape[0], tallies.shape[1], row_count * NZ)
    summed = lax.psum_scatter(
        flat_tallies.astype(jnp.bfloat16), "member", scatter_dimension=2, tiled=True
    ).astype(jnp.float32)
    return summed / total_members


def solution(mesh):
    in_specs = (P("member", "tile", None),)
    out_specs = P(None, "tile", "member")
    return jax.shard_map(local, mesh=mesh, in_specs=in_specs, out_specs=out_specs, check_vma=False)
```

profile of v0, /device:TPU:0, one launch (start us, length us, event | category | flops | bytes accessed | tf_op | source)
XLA Modules:
  0.0 67.8 jit_solution(12946390093152720853)
XLA Ops:
  6.5 1.0 %convert_element_type.91 = bf16[2,6,3072]{2,0,1:T(2,128)(2,1)S(1)} convert(f32[2,6,3072]{2,0,1:T(2,128)} %param.1) | non-fusion elementwise | flops 36864 | bytes 221184 | tf_op jit(solution)/shard_map/convert_element_type | solution.py:67
  7.5 0.1 convert_element_type.92
  7.6 4.9 %collective-permute-start = (bf16[2,1,16,192]{3,2,0,1:T(8,128)(2,1)S(1)}, bf16[2,1,16,192]{3,2,0,1:T(8,128)(2,1)S(1)}, u32[]{:S(2)}, u32[]{:S(2)}) collective-permute-start(bf16[2,1,16,192]{3,2,0,1:T(8,128)(2,1)S(1)} %get-tuple-element.43), channel_id=1, source_target_pairs={{0,1},{1,2},{2,3},{3,4},{4,5},{5,6},{6,7},{8,9},{9,10},{10,11},{11... | collective-permute-start | bytes 36872 | tf_op jit(solution)/shard_map/ppermute | solution.py:22
  12.5 1.3 %collective-permute-start.1 = (bf16[2,1,16,192]{3,2,0,1:T(8,128)(2,1)S(1)}, bf16[2,1,16,192]{3,2,0,1:T(8,128)(2,1)S(1)}, u32[]{:S(2)}, u32[]{:S(2)}) collective-permute-start(bf16[2,1,16,192]{3,2,0,1:T(8,128)(2,1)S(1)} %get-tuple-element.44), channel_id=1, source_target_pairs={{1,0},{2,1},{3,2},{4,3},{5,4},{6,5},{7,6},{9,8},{10,9},{11,10},{12... | collective-permute-start | bytes 36872 | tf_op jit(solution)/shard_map/ppermute | solution.py:23
  13.9 4.2 %collective-permute-done.1 = bf16[2,1,16,192]{3,2,0,1:T(8,128)(2,1)S(1)} collective-permute-done((bf16[2,1,16,192]{3,2,0,1:T(8,128)(2,1)S(1)}, bf16[2,1,16,192]{3,2,0,1:T(8,128)(2,1)S(1)}, u32[]{:S(2)}, u32[]{:S(2)}) %collective-permute-start.1) | collective-permute-done | bytes 12320 | tf_op jit(solution)/shard_map/ppermute | solution.py:23
  18.2 1.2 %or_or_fusion.4 = (pred[2,6,16,192]{3,2,0,1:T(8,128)(4,1)S(1)}, pred[2,6,16,192]{3,2,0,1:T(8,128)(4,1)S(1)}, pred[2,6,16,192]{3,2,0,1:T(8,128)(4,1)S(1)}, pred[2...) fusion(f32[2,8,16,192]{3,2,0,1:T(8,128)S(1)} %convert_select_fusion), kind=kLoop, calls=%fused_computation.109 | loop fusion | flops 3133440 | bytes 1257472 | tf_op jit(solution)/shard_map/or | solution.py:50
  20.1 0.1 stack.109
  20.2 0.3 or_or_fusion.3
  20.8 0.1 stack.115
  20.9 0.3 or_or_fusion.2
  21.5 0.1 stack.118
  21.7 0.3 or_or_fusion.1
  22.3 0.1 stack.121
  22.4 0.7 %not_and_fusion.1 = (pred[2,6,16,192]{3,2,0,1:T(8,128)(4,1)S(1)}, pred[2,6,16,192]{3,2,0,1:T(8,128)(4,1)S(1)}, pred[2,6,16,192]{3,2,0,1:T(8,128)(4,1)S(1)}, pred...) fusion(f32[2,6,16,192]{3,2,0,1:T(8,128)S(1)} %get-tuple-element, ...), kind=kLoop, calls=%fused_computation.80 | loop fusion | flops 1990656 | bytes 1269760 | tf_op jit(solution)/shard_map/and | solution.py:48
  23.1 0.4 convert_reduce_fusion
  23.8 0.1 stack.132
  24.0 0.1 stack.126
  24.1 0.1 stack.127
  24.4 0.1 stack.130
  24.6 0.1 stack.131
  24.9 0.1 stack.125
  25.1 7.1 %stack.107 = bf16[26,6,3072]{2,0,1:T(8,128)(2,1)} concatenate(bf16[1,6,3072]{2,0,1:T(2,128)(2,1)S(1)} %stack.108, bf16[1,6,3072]{2,0,1:T(2,128)(2,1)S(1)} %stack.109, bf16[1,6,3072]{2,0,1:T(2,128)(2,1)S(1)} %stack.110, bf16[1,6,3072]{2,0,1:T(2,128)(2,1)S(1)} %stack.111, bf16[1,6,3072]{2,0,1:T(2,128)(2,1)S(1)} %stack.112, bf16[1,6,3072]{2,0,1:T(2,128)(2,1)S(1)} %stack.113, ...), dimensions={0} | concatenate | bytes 1916928 | tf_op jit(solution)/shard_map/stack | solution.py:51
  32.2 27.0 %reduce-scatter.2.cloned.1.call-done = bf16[26,6,768]{2,0,1:T(8,128)(2,1)} async-done(((bf16[26,6,3072]{2,0,1:T(8,128)(2,1)}), bf16[26,6,768]{2,0,1:T(8,128)(2,1)}) %reduce-scatter.2.cloned.1.call-update) | async-done | bytes 239632 | tf_op jit(solution)/shard_map/reduce_scatter | solution.py:72
  59.2 1.8 %convert_multiply_fusion = f32[26,6,768]{2,0,1:T(8,128)} fusion(bf16[26,6,768]{2,0,1:T(8,128)(2,1)} %reduce-scatter.2.cloned.1.call-done), kind=kLoop, calls=%fused_computation.24 | loop fusion | flops 239616 | bytes 718848 | tf_op jit(solution)/shard_map/div | solution.py:75
  (33 shorter events, 2.5 us)
Async XLA Ops:
  6.5 52.6 %reduce-scatter.2.cloned.1.call-start = ((), (), s32[]{:S(2)}) async-start(), calls=%async_computation.1 | async-start | bytes 1474560 | tf_op jit(solution)/shard_map/reduce_scatter | solution.py:72
  7.6 6.3 %collective-permute-start = (bf16[2,1,16,192]{3,2,0,1:T(8,128)(2,1)S(1)}, bf16[2,1,16,192]{3,2,0,1:T(8,128)(2,1)S(1)}, u32[]{:S(2)}, u32[]{:S(2)}) collective-permute-start(bf16[2,1,16,192]{3,2,0,1:T(8,128)(2,1)S(1)} %get-tuple-element.43), channel_id=1, source_target_pairs={{0,1},{1,2},{2,3},{3,4},{4,5},{5,6},{6,7},{8,9},{9,10},{10,11},{11... | collective-permute-start | bytes 36872 | tf_op jit(solution)/shard_map/ppermute | solution.py:22
  12.5 5.6 %collective-permute-start.1 = (bf16[2,1,16,192]{3,2,0,1:T(8,128)(2,1)S(1)}, bf16[2,1,16,192]{3,2,0,1:T(8,128)(2,1)S(1)}, u32[]{:S(2)}, u32[]{:S(2)}) collective-permute-start(bf16[2,1,16,192]{3,2,0,1:T(8,128)(2,1)S(1)} %get-tuple-element.44), channel_id=1, source_target_pairs={{1,0},{2,1},{3,2},{4,3},{5,4},{6,5},{7,6},{9,8},{10,9},{11,10},{12... | collective-permute-start | bytes 36872 | tf_op jit(solution)/shard_map/ppermute | solution.py:23
Sparse Core Ops, SparseCore 0:
  32.3 26.8 reduce-scatter.1
where the time goes:
time: 68 us; the launch traced here: 67.8 us
  waiting for transfers between devices  31.3 us (46%)
  between operations  13.7 us (20%)
  local copies, waits for them, and re-layouts  10.1 us (15%)
  other arithmetic  6.53 us (10%)
  starting transfers between devices  6.17 us (9%)
    reduce_scatter x1, waiting for transfers between devices, local(): lax.psum_scatter(flat_tallies.astype(jnp.bfloat16), 'member', scatter_dim...  27 us
    another operation x27, local copies, waits for them, and re-layouts, direction_counts(): return jnp.stack(tallies)  10 us
    ppermute x1, starting transfers between devices, with_halo(): before = lax.ppermute(last, axis, up)  4.87 us
    ppermute x1, waiting for transfers between devices, with_halo(): after = lax.ppermute(leading, axis, down)  4.21 us
    or x4, other arithmetic, direction_counts(): claimed = claimed | chosen  2.06 us
    div x1, other arithmetic, local(): return summed / total_members  1.83 us
  transfers between devices with their start and end apart: 3, of which 3 were waited for; matrix products, arithmetic and copies ran while one was open for 0% of the time, Pallas kernels for 0%

commit v1 on v0

v1 whole, which is shorter than its diff:
```python
import functools

import jax
import jax.numpy as jnp
from jax import lax
from jax.experimental import pallas as pl
from jax.experimental.pallas import tpu as pltpu
from jax.sharding import PartitionSpec as P

NZ = 192
LANES = 128
EDGE = 3
PAD = 64.0
FAR = 4096.0
VMEM = pl.BlockSpec(memory_space=pltpu.VMEM)
PARAMS = pltpu.CompilerParams(vmem_limit_bytes=8 << 20)


def permute(value, pairs):
    return lax.ppermute(value, ("member", "tile"), pairs)


def pairs_of(members, tiles, partner):
    pairs = []
    for m in range(members):
        for t in range(tiles):
            to_m, to_t = partner(m, t)
            pairs.append((m * tiles + t, to_m * tiles + to_t))
    return pairs


def even_partner(members, tiles):
    return pairs_of(members, tiles, lambda m, t: (m, t ^ 1))


def odd_partner(members, tiles):
    def partner(m, t):
        if t == 0 or t == tiles - 1:
            return m ^ (members // 2), t
        return m, (t + 1 if t % 2 else t - 1)

    return pairs_of(members, tiles, partner)


def cut_kernel(mloc, width, step, members, src, *rest):
    outs, padded = rest[:members], rest[members]
    planes, rows = src.shape[0], src.shape[1]
    lead = 8
    assert lead >= EDGE * mloc
    me = lax.axis_index("member")
    for p in range(planes):
        padded[p, 0:lead, :] = jnp.full((lead, LANES), PAD, jnp.float32)
        padded[p, lead : lead + rows, :] = src[p]
        padded[p, lead + rows : lead + rows + lead, :] = jnp.full((lead, LANES), PAD, jnp.float32)
    for k in range(members):
        base = (me ^ k) * (step * mloc) + lead - EDGE * mloc
        for p in range(planes):
            for i in range(mloc):
                cut = padded[p, pl.ds(base + i, width, stride=mloc), :]
                outs[k][p, i * width : (i + 1) * width, :] = cut.astype(jnp.bfloat16)


def edge_kernel(members, *refs):
    bufs, (send_even, send_odd) = refs[:members], refs[members:]
    planes, rows = bufs[0].shape[0], bufs[0].shape[1]
    odd = lax.axis_index("tile") % 2
    for k in range(members):
        send_even[k * rows : (k + 1) * rows, :] = bufs[k][(planes - 1) * (1 - odd)]
        send_odd[k * rows : (k + 1) * rows, :] = bufs[k][(planes - 1) * odd]


def count_kernel(members, mloc, width, step, *refs):
    bufs = refs[:members]
    got_even, got_odd, out, stage = refs[members:]
    planes, rows = bufs[0].shape[0], bufs[0].shape[1]
    total = members * mloc
    tile, tiles = lax.axis_index("tile"), lax.axis_size("tile")
    odd = tile % 2
    for k in range(members):
        for p in range(planes):
            stage[p + 1, k * rows : (k + 1) * rows, :] = bufs[k][p].astype(jnp.float32)
    stage[(planes + 1) * (1 - odd)] = got_even[...].astype(jnp.float32)
    stage[(planes + 1) * odd] = got_odd[...].astype(jnp.float32)

    @pl.when(tile == 0)
    def _():
        stage[0] = jnp.full(stage.shape[1:], PAD, jnp.float32)

    @pl.when(tile == tiles - 1)
    def _():
        stage[planes + 1] = jnp.full(stage.shape[1:], PAD, jnp.float32)

    lane = lax.broadcasted_iota(jnp.int32, (8, LANES), 1)
    sub = lax.broadcasted_iota(jnp.int32, (8, LANES), 0)
    low, first, last = lane < 64, lane == 0, lane == LANES - 1
    at64, at63 = lane == 64, lane == 63
    groups = -(-out.shape[1] // 8)

    def plane_keys(p, group):
        value = {
            j: stage[p, pl.ds(group * 8 * width + j, 8, stride=width), :] * 32.0
            for j in range(EDGE - 2, EDGE + step + 2)
        }
        keys = {}
        for j, here in value.items():
            before = pltpu.roll(here, 1, 1)
            after = pltpu.roll(here, LANES - 1, 1)
            phase = j % 3
            if phase == 0:
                before = jnp.where(first, FAR, before)
            elif j - 1 in value:
                before = jnp.where(first, pltpu.roll(value[j - 1], 1, 1), before)
            if phase == 2:
                after = jnp.where(last, FAR, after)
            elif j + 1 in value:
                after = jnp.where(last, pltpu.roll(value[j + 1], LANES - 1, 1), after)
            if phase == 1:
                before = jnp.where(at64, FAR, before)
                after = jnp.where(at63, FAR, after)
            keys[j] = jnp.minimum(jnp.minimum(before, here + 1.0), after + 2.0)
        turned = {j: pltpu.roll(key, 64, 1) for j, key in keys.items()}
        row_before = {
            j: jnp.where(low, turned[j - 2], turned[j - 1]) for j in range(EDGE, EDGE + step + 3)
        }
        result = []
        for j in range(EDGE, EDGE + step):
            key = jnp.minimum(row_before[j], keys[j] + 3.0)
            result.append((jnp.minimum(key, row_before[j + 3] + 6.0), value[j]))
        return result

    for group in range(total // 8):
        layers = [plane_keys(p, group) for p in range(planes + 2)]
        for p in range(planes):
            for j in range(step):
                best = jnp.minimum(layers[p][j][0], layers[p + 1][j][0] + 9.0)
                best = jnp.minimum(best, layers[p + 2][j][0] + 18.0)
                found = best < layers[p + 1][j][1]
                code = best.astype(jnp.int32) & 31
                code = jnp.where(code > 13, code - 1, code)
                bit = jnp.where(found, jnp.int32(1) << ((code & 7) * 4), 0)
                kind = code >> 3
                for g in range(groups):
                    word = jnp.where(kind == g, bit, 0)
                    word = word + pltpu.roll(word, 4, 0)
                    word = word + pltpu.roll(word, 2, 0)
                    word = word + pltpu.roll(word, 1, 0)
                    share = ((word >> (sub * 4)) & 15).astype(jnp.float32) * (1.0 / total)
                    n = min(8, out.shape[1] - 8 * g)
                    at = (p, slice(8 * g, 8 * g + n), slice(j * LANES, (j + 1) * LANES))
                    if group == 0:
                        out[at] = share[:n]
                    else:
                        out[at] = out[at] + share[:n]


def local(members, tiles, fields):
    mloc, planes, cols = fields.shape
    step = cols // members // LANES
    width = step + 2 * EDGE
    spread = cols // LANES
    view = fields.reshape(mloc, planes, spread, LANES).transpose(1, 2, 0, 3)
    view = view.reshape(planes, spread * mloc, LANES)
    rows = mloc * width
    cuts = pl.pallas_call(
        functools.partial(cut_kernel, mloc, width, step, members),
        out_shape=[jax.ShapeDtypeStruct((planes, rows, LANES), jnp.bfloat16)] * members,
        in_specs=[VMEM],
        out_specs=[VMEM] * members,
        scratch_shapes=[pltpu.VMEM((planes, spread * mloc + 16, LANES), jnp.float32)],
        compiler_params=PARAMS,
        name="cut",
    )(view)
    bufs = [cuts[0]] + [
        permute(cuts[k], pairs_of(members, tiles, lambda m, t: (m ^ k, t))) for k in range(1, members)
    ]
    edge = jax.ShapeDtypeStruct((members * rows, LANES), jnp.bfloat16)
    send_even, send_odd = pl.pallas_call(
        functools.partial(edge_kernel, members),
        out_shape=[edge, edge],
        in_specs=[VMEM] * members,
        out_specs=[VMEM] * 2,
        compiler_params=PARAMS,
        name="edge",
    )(*bufs)
    got_even = permute(send_even, even_partner(members, tiles))
    got_odd = permute(send_odd, odd_partner(members, tiles))
    out = pl.pallas_call(
        functools.partial(count_kernel, members, mloc, width, step),
        out_shape=jax.ShapeDtypeStruct((planes, 26, step * LANES), jnp.float32),
        in_specs=[VMEM] * (members + 2),
        out_specs=VMEM,
        scratch_shapes=[pltpu.VMEM((planes + 2, members * rows, LANES), jnp.float32)],
        compiler_params=PARAMS,
        name="count",
    )(*bufs, got_even, got_odd)
    return out.transpose(1, 0, 2)


def solution(mesh):
    sizes = dict(mesh.shape)
    in_specs = (P("member", "tile", None),)
    out_specs = P(None, "tile", "member")
    body = functools.partial(local, sizes["member"], sizes["tile"])
    return jax.shard_map(body, mesh=mesh, in_specs=in_specs, out_specs=out_specs, check_vma=False)
```

time: 68 us -> 14.7 us (0.22)
  waiting for transfers between devices: 31.3 us -> 6.24 us
  between operations: 13.7 us -> 0.01 us
  local copies, waits for them, and re-layouts: 10.1 us -> 0.91 us
  other arithmetic: 6.53 us -> 0 us
  Pallas kernels: 0 us -> 1.74 us
    reduce_scatter x1 -> x0, waiting for transfers between devices: 27 us -> none  [local(): lax.psum_scatter(flat_tallies.astype(jnp.bfloat16), 'member', scatter_dim...]
    another operation x27 -> x0, local copies, waits for them, and re-layouts: 10 us -> none  [direction_counts(): return jnp.stack(tallies)]
    or x5 -> x0, other arithmetic: 2.07 us -> none  [the longest x4 2.06 us: direction_counts(): claimed = claimed | chosen]
    ppermute x2 -> x5, waiting for transfers between devices: 4.31 us -> 6.24 us  [permute(): return lax.ppermute(value, ('member', 'tile'), pairs)]
    div x1 -> x0, other arithmetic: 1.83 us -> none  [local(): return summed / total_members]
    pallas_call x0 -> x3, Pallas kernels: none -> 1.74 us  [the longest x1 1.67 us: local(): pl.pallas_call(functools.partial(count_kernel, members, mloc, width, step...]
    convert_element_type x1 -> x0, other arithmetic: 0.96 us -> none  [local(): shaped.astype(jnp.bfloat16)]
    unnamed x0 -> x2, local copies, waits for them, and re-layouts: none -> 0.91 us
  transfers between devices with their start and end apart: 3 -> 5, of which waited for: 3 -> 4; matrix products, arithmetic and copies ran while one was open for 0% -> 0% of each run, Pallas kernels for 0% -> 0%
where the time goes in v1:
time: 14.7 us; the launch traced here: 14.5 us
  waiting for transfers between devices  6.24 us (42%)
  starting transfers between devices  5.62 us (38%)
  Pallas kernels  1.74 us (12%)
  local copies, waits for them, and re-layouts  0.91 us (6%)
    ppermute x5, waiting for transfers between devices, permute(): return lax.ppermute(value, ('member', 'tile'), pairs)  6.24 us
    ppermute x5, starting transfers between devices, permute(): return lax.ppermute(value, ('member', 'tile'), pairs)  5.62 us
    pallas_call x1, Pallas kernels, local(): pl.pallas_call(functools.partial(count_kernel, members, mloc, width, step...  1.67 us
    unnamed x2, local copies, waits for them, and re-layouts  0.91 us
  transfers between devices with their start and end apart: 5, of which 4 were waited for; matrix products, arithmetic and copies ran while one was open for 0% of the time, Pallas kernels for 0%

profile of v1, /device:TPU:0, one launch (start us, length us, event | category | flops | bytes accessed | tf_op | source)
XLA Modules:
  0.0 14.5 jit_solution(16077428213780206844)
XLA Ops:
  0.0 0.0 copy-start
  0.0 0.9 %copy-done = f32[2,6,3072]{2,0,1:T(2,128)S(1)} copy-done((f32[2,6,3072]{2,0,1:T(2,128)S(1)}, f32[2,6,3072]{2,0,1:T(2,128)}, u32[]{:S(2)}) %copy-start) | copy-done | bytes 147480
  0.9 0.1 cut.1
  1.0 0.5 %collective-permute-start = (bf16[6,24,128]{2,1,0:T(8,128)(2,1)S(1)}, bf16[6,24,128]{2,1,0:T(8,128)(2,1)S(1)}, u32[]{:S(2)}, u32[]{:S(2)}) collective-permute-start(bf16[6,24,128]{2,1,0:T(8,128)(2,1)S(1)} %get-tuple-element.12), channel_id=1, source_target_pairs={{0,8},{1,9},{2,10},{3,11},{4,12},{5,13},{6,14},{7,15},{8,0},{9,1},... | collective-permute-start | bytes 110600 | tf_op jit(solution)/shard_map/ppermute | solution.py:20
  1.5 2.6 %collective-permute-start.1 = (bf16[6,24,128]{2,1,0:T(8,128)(2,1)S(1)}, bf16[6,24,128]{2,1,0:T(8,128)(2,1)S(1)}, u32[]{:S(2)}, u32[]{:S(2)}) collective-permute-start(bf16[6,24,128]{2,1,0:T(8,128)(2,1)S(1)} %get-tuple-element.13), channel_id=1, source_target_pairs={{0,16},{1,17},{2,18},{3,19},{4,20},{5,21},{6,22},{7,23},{8,24},{9,... | collective-permute-start | bytes 110600 | tf_op jit(solution)/shard_map/ppermute | solution.py:20
  4.1 0.1 collective-permute-start.2
  4.1 0.0 collective-permute-done.refs_1_
  4.1 2.0 %collective-permute-done.1.refs_2_ = bf16[6,24,128]{2,1,0:T(8,128)(2,1)S(1)} collective-permute-done((bf16[6,24,128]{2,1,0:T(8,128)(2,1)S(1)}, bf16[6,24,128]{2,1,0:T(8,128)(2,1)S(1)}, u32[]{:S(2)}, u32[]{:S(2)}) %collective-permute-start.1) | collective-permute-done | bytes 36896 | tf_op jit(solution)/shard_map/ppermute | solution.py:20
  6.1 1.4 %collective-permute-done.2.refs_3_ = bf16[6,24,128]{2,1,0:T(8,128)(2,1)S(1)} collective-permute-done((bf16[6,24,128]{2,1,0:T(8,128)(2,1)S(1)}, bf16[6,24,128]{2,1,0:T(8,128)(2,1)S(1)}, u32[]{:S(2)}, u32[]{:S(2)}) %collective-permute-start.2) | collective-permute-done | bytes 36896 | tf_op jit(solution)/shard_map/ppermute | solution.py:20
  7.5 1.5 %collective-permute-start.3 = (bf16[96,128]{1,0:T(8,128)(2,1)S(1)}, bf16[96,128]{1,0:T(8,128)(2,1)S(1)}, u32[]{:S(2)}, u32[]{:S(2)}) collective-permute-start(bf16[96,128]{1,0:T(8,128)(2,1)S(1)} %get-tuple-element.15), channel_id=1, source_target_pairs={{0,1},{1,0},{2,3},{3,2},{4,5},{5,4},{6,7},{7,6},{8,9},{9,8},{10,11... | collective-permute-start | bytes 73736 | tf_op jit(solution)/shard_map/ppermute | solution.py:20
  9.0 1.0 %collective-permute-start.4 = (bf16[96,128]{1,0:T(8,128)(2,1)S(1)}, bf16[96,128]{1,0:T(8,128)(2,1)S(1)}, u32[]{:S(2)}, u32[]{:S(2)}) collective-permute-start(bf16[96,128]{1,0:T(8,128)(2,1)S(1)} %get-tuple-element.16), channel_id=1, source_target_pairs={{0,16},{1,2},{2,1},{3,4},{4,3},{5,6},{6,5},{7,23},{8,24},{9,10},{1... | collective-permute-start | bytes 73736 | tf_op jit(solution)/shard_map/ppermute | solution.py:20
  10.0 1.4 %collective-permute-done.3.refs_4_ = bf16[96,128]{1,0:T(8,128)(2,1)S(1)} collective-permute-done((bf16[96,128]{1,0:T(8,128)(2,1)S(1)}, bf16[96,128]{1,0:T(8,128)(2,1)S(1)}, u32[]{:S(2)}, u32[]{:S(2)}) %collective-permute-start.3) | collective-permute-done | bytes 24608 | tf_op jit(solution)/shard_map/ppermute | solution.py:20
  11.3 1.5 %collective-permute-done.4.refs_5_ = bf16[96,128]{1,0:T(8,128)(2,1)S(1)} collective-permute-done((bf16[96,128]{1,0:T(8,128)(2,1)S(1)}, bf16[96,128]{1,0:T(8,128)(2,1)S(1)}, u32[]{:S(2)}, u32[]{:S(2)}) %collective-permute-start.4) | collective-permute-done | bytes 24608 | tf_op jit(solution)/shard_map/ppermute | solution.py:20
  12.8 1.7 %count.1 = f32[6,26,768]{2,1,0:T(8,128)} custom-call(bf16[6,24,128]{2,1,0:T(8,128)(2,1)S(1)} %get-tuple-element.11.refs_0_, bf16[6,24,128]{2,1,0:T(8,128)(2,1)S(1)} %collective-permute-done.refs_1_, bf16[6,24,128]{2,1,0:T(8,128)(2,1)S(1)} %collective-permute-done.1.refs_2_, bf16[6,24,128]{2,1,0:T(8,128)(2,1)S(1)} %collective-permute-done.2.refs_3_, ...), custom_call_target="tpu_custom_call" | custom-call | tf_op jit(solution)/shard_map/count/pallas_call | solution.py:187
  (1 shorter events, 0.0 us)
Async XLA Ops:
  0.0 0.9 %copy-start = (f32[2,6,3072]{2,0,1:T(2,128)S(1)}, f32[2,6,3072]{2,0,1:T(2,128)}, u32[]{:S(2)}) copy-start(f32[2,6,3072]{2,0,1:T(2,128)} %param.1) | copy-start | bytes 442372
  1.0 3.2 %collective-permute-start = (bf16[6,24,128]{2,1,0:T(8,128)(2,1)S(1)}, bf16[6,24,128]{2,1,0:T(8,128)(2,1)S(1)}, u32[]{:S(2)}, u32[]{:S(2)}) collective-permute-start(bf16[6,24,128]{2,1,0:T(8,128)(2,1)S(1)} %get-tuple-element.12), channel_id=1, source_target_pairs={{0,8},{1,9},{2,10},{3,11},{4,12},{5,13},{6,14},{7,15},{8,0},{9,1},... | collective-permute-start | bytes 110600 | tf_op jit(solution)/shard_map/ppermute | solution.py:20
  1.5 4.6 %collective-permute-start.1 = (bf16[6,24,128]{2,1,0:T(8,128)(2,1)S(1)}, bf16[6,24,128]{2,1,0:T(8,128)(2,1)S(1)}, u32[]{:S(2)}, u32[]{:S(2)}) collective-permute-start(bf16[6,24,128]{2,1,0:T(8,128)(2,1)S(1)} %get-tuple-element.13), channel_id=1, source_target_pairs={{0,16},{1,17},{2,18},{3,19},{4,20},{5,21},{6,22},{7,23},{8,24},{9,... | collective-permute-start | bytes 110600 | tf_op jit(solution)/shard_map/ppermute | solution.py:20
  4.1 3.4 %collective-permute-start.2 = (bf16[6,24,128]{2,1,0:T(8,128)(2,1)S(1)}, bf16[6,24,128]{2,1,0:T(8,128)(2,1)S(1)}, u32[]{:S(2)}, u32[]{:S(2)}) collective-permute-start(bf16[6,24,128]{2,1,0:T(8,128)(2,1)S(1)} %get-tuple-element.14), channel_id=1, source_target_pairs={{0,24},{1,25},{2,26},{3,27},{4,28},{5,29},{6,30},{7,31},{8,16},{9,... | collective-permute-start | bytes 110600 | tf_op jit(solution)/shard_map/ppermute | solution.py:20
  7.5 3.8 %collective-permute-start.3 = (bf16[96,128]{1,0:T(8,128)(2,1)S(1)}, bf16[96,128]{1,0:T(8,128)(2,1)S(1)}, u32[]{:S(2)}, u32[]{:S(2)}) collective-permute-start(bf16[96,128]{1,0:T(8,128)(2,1)S(1)} %get-tuple-element.15), channel_id=1, source_target_pairs={{0,1},{1,0},{2,3},{3,2},{4,5},{5,4},{6,7},{7,6},{8,9},{9,8},{10,11... | collective-permute-start | bytes 73736 | tf_op jit(solution)/shard_map/ppermute | solution.py:20
  9.0 3.8 %collective-permute-start.4 = (bf16[96,128]{1,0:T(8,128)(2,1)S(1)}, bf16[96,128]{1,0:T(8,128)(2,1)S(1)}, u32[]{:S(2)}, u32[]{:S(2)}) collective-permute-start(bf16[96,128]{1,0:T(8,128)(2,1)S(1)} %get-tuple-element.16), channel_id=1, source_target_pairs={{0,16},{1,2},{2,1},{3,4},{4,3},{5,6},{6,5},{7,23},{8,24},{9,10},{1... | collective-permute-start | bytes 73736 | tf_op jit(solution)/shard_map/ppermute | solution.py:20

commit v2 on v0

v2 whole, which is shorter than its diff:
```python
import functools

import jax
import jax.numpy as jnp
from jax import lax
from jax.experimental import pallas as pl
from jax.experimental.pallas import tpu as pltpu
from jax.sharding import PartitionSpec as P

NZ = 192
LANES = 128
EDGE = 2
LEAD = 8
PAD = 64.0
FAR = 4096.0
VMEM = pl.BlockSpec(memory_space=pltpu.VMEM)
ANY = pl.BlockSpec(memory_space=pl.ANY)
PARAMS = pltpu.CompilerParams(vmem_limit_bytes=8 << 20)


def permute(value, members, tiles, partner):
    pairs = []
    for m in range(members):
        for t in range(tiles):
            to_m, to_t = partner(m, t)
            pairs.append((m * tiles + t, to_m * tiles + to_t))
    return lax.ppermute(value, ("member", "tile"), pairs)


def beside(q, members, tiles, m, t):
    if m % 2 == 0:
        return m ^ (2 * q), t ^ 1
    if t == 0 or t == tiles - 1:
        return m ^ (2 * q if q else members // 2), t
    return m ^ (2 * q), (t + 1 if t % 2 else t - 1)


def edge_side():
    return (lax.axis_index("member") + lax.axis_index("tile")) % 2


def load_kernel(src, out):
    planes, rows = src.shape[0], src.shape[1]
    fill = jnp.full((planes, LEAD, LANES), PAD, jnp.float32)
    out[:, 0:LEAD, :] = fill
    out[:, LEAD : LEAD + rows, :] = src[...]
    out[:, LEAD + rows : LEAD + rows + LEAD, :] = fill


def spread_kernel(theirs, ours, both):
    core = lax.axis_index("member") % 2
    both[core] = ours[...]
    load_kernel(theirs, both.at[1 - core])


def window(both, mloc, p, start, size):
    base = start * mloc + LEAD - EDGE * mloc
    parts = [both[c, p, pl.ds(base + i, size, stride=mloc), :] for c in range(2) for i in range(mloc)]
    return jnp.concatenate(parts, axis=0).astype(jnp.bfloat16)


def edges_kernel(mloc, wide, step, theirs, ours, both, *edges):
    spread_kernel(theirs, ours, both)
    pair = lax.axis_index("member") // 2
    plane = (ours.shape[0] - 1) * (1 - edge_side())
    for q, edge in enumerate(edges):
        edge[...] = window(both, mloc, plane, (pair ^ q) * (2 * step), wide)


def blocks_kernel(mloc, width, step, both, *blocks):
    me = lax.axis_index("member")
    for q, block in enumerate(blocks):
        for p in range(block.shape[0]):
            block[p] = window(both, mloc, p, (me ^ (2 * q)) * step, width)


def join_kernel(*refs):
    bufs, out = refs[:-1], refs[-1]
    rows = bufs[0].shape[0]
    for k, buf in enumerate(bufs):
        out[k * rows : (k + 1) * rows, :] = buf[...]


def keys_of(stage, p, group, width, step, start):
    lane = lax.broadcasted_iota(jnp.int32, (8, LANES), 1)
    low, first, last = lane < 64, lane == 0, lane == LANES - 1
    at64, at63 = lane == 64, lane == 63
    base = group * 8 * width + start
    value = {
        j: stage[p, pl.ds(base + j, 8, stride=width), :] * 32.0
        for j in range(EDGE - 2, EDGE + step + 2)
    }
    keys = {}
    for j, here in value.items():
        before = pltpu.roll(here, 1, 1)
        after = pltpu.roll(here, LANES - 1, 1)
        phase = (j - EDGE) % 3
        if phase == 0:
            before = jnp.where(first, FAR, before)
        elif j - 1 in value:
            before = jnp.where(first, pltpu.roll(value[j - 1], 1, 1), before)
        if phase == 2:
            after = jnp.where(last, FAR, after)
        elif j + 1 in value:
            after = jnp.where(last, pltpu.roll(value[j + 1], LANES - 1, 1), after)
        if phase == 1:
            before = jnp.where(at64, FAR, before)
            after = jnp.where(at63, FAR, after)
        keys[j] = jnp.minimum(jnp.minimum(before, here + 1.0), after + 2.0)
    turned = {j: pltpu.roll(key, 64, 1) for j, key in keys.items()}
    row_before = {
        j: jnp.where(low, turned[j - 2], turned[j - 1]) for j in range(EDGE, EDGE + step + 3)
    }
    result = []
    for j in range(EDGE, EDGE + step):
        key = jnp.minimum(row_before[j], keys[j] + 3.0)
        result.append(jnp.minimum(key, row_before[j + 3] + 6.0))
    return result, [value[j] for j in range(EDGE, EDGE + step)]


def tally(best, value, out, p, j, add, total):
    sub = lax.broadcasted_iota(jnp.int32, (8, LANES), 0)
    code = best.astype(jnp.int32) & 31
    code = jnp.where(code > 13, code - 1, code)
    bit = jnp.where(best < value, jnp.int32(1) << ((code & 7) * 4), 0)
    kind = code >> 3
    for g in range(-(-out.shape[1] // 8)):
        word = jnp.where(kind == g, bit, 0)
        word = word + pltpu.roll(word, 4, 0)
        word = word + pltpu.roll(word, 2, 0)
        word = word + pltpu.roll(word, 1, 0)
        share = ((word >> (sub * 4)) & 15).astype(jnp.float32) * (1.0 / total)
        n = min(8, out.shape[1] - 8 * g)
        at = (p, slice(8 * g, 8 * g + n), slice(j * LANES, (j + 1) * LANES))
        out[at] = out[at] + share[:n] if add else share[:n]


def inner_kernel(width, step, total, *refs):
    blocks, (out, part, stage, tile_out, sem) = refs[:-5], refs[-5:]
    planes, rows = blocks[0].shape[0], blocks[0].shape[1]
    for q, block in enumerate(blocks):
        for p in range(planes):
            stage[p, q * rows : (q + 1) * rows, :] = block[p].astype(jnp.float32)
    for group in range(total // 8):
        layers = [keys_of(stage, p, group, width, step, 0) for p in range(planes)]
        for j in range(step):
            key = [layer[0][j] for layer in layers]
            value = [layer[1][j] for layer in layers]
            part[group, 0, j] = jnp.minimum(key[0] + 9.0, key[1] + 18.0)
            part[group, 1, j] = value[0]
            part[group, 2, j] = jnp.minimum(key[planes - 2], key[planes - 1] + 9.0)
            part[group, 3, j] = value[planes - 1]
            for p in range(1, planes - 1):
                best = jnp.minimum(jnp.minimum(key[p - 1], key[p] + 9.0), key[p + 1] + 18.0)
                tally(best, value[p], tile_out, p - 1, j, group > 0, total)
    copy = pltpu.make_async_copy(tile_out, out.at[pl.ds(1, planes - 2)], sem)
    copy.start()
    copy.wait()


def outer_kernel(wide, step, total, got, other, part, partial_out, out, stage, tile_out, sem):
    planes = out.shape[0]
    tile, tiles = lax.axis_index("tile"), lax.axis_size("tile")
    side = edge_side()
    start = (lax.axis_index("member") % 2) * step
    stage[1 - side] = got[...].astype(jnp.float32)
    stage[side] = other[...].astype(jnp.float32)

    @pl.when(tile == 0)
    def _():
        stage[0] = jnp.full(stage.shape[1:], PAD, jnp.float32)

    @pl.when(tile == tiles - 1)
    def _():
        stage[1] = jnp.full(stage.shape[1:], PAD, jnp.float32)

    for end, (plane, bias) in enumerate(((0, 0.0), (planes - 1, 18.0))):
        for group in range(total // 8):
            keys, _ = keys_of(stage, end, group, wide, step, start)
            for j in range(step):
                best = jnp.minimum(part[group, 2 * end, j], keys[j] + bias)
                tally(best, part[group, 2 * end + 1, j], tile_out, end, j, group > 0, total)
        pltpu.make_async_copy(tile_out.at[end], out.at[plane], sem.at[end]).start()
    for end, plane in enumerate((0, planes - 1)):
        pltpu.make_async_copy(tile_out.at[end], out.at[plane], sem.at[end]).wait()


def local(members, tiles, fields):
    mloc, planes, cols = fields.shape
    step = cols // members // LANES
    width, wide = step + 2 * EDGE, 2 * step + 2 * EDGE
    spread = cols // LANES
    assert LEAD >= EDGE * mloc
    total = members * mloc
    half = members // 2
    bf16, f32 = jnp.bfloat16, jnp.float32

    def swap(value):
        return permute(value, members, tiles, lambda m, t: (m ^ 1, t))

    view = fields.reshape(mloc, planes, spread, LANES).transpose(1, 2, 0, 3)
    view = view.reshape(planes, spread * mloc, LANES)
    padded = (planes, spread * mloc + 2 * LEAD, LANES)
    ours = pl.pallas_call(
        load_kernel,
        out_shape=jax.ShapeDtypeStruct(padded, f32),
        in_specs=[VMEM],
        out_specs=VMEM,
        compiler_params=PARAMS,
        name="load",
    )(view)
    both, *edges = pl.pallas_call(
        functools.partial(edges_kernel, mloc, wide, step),
        out_shape=[jax.ShapeDtypeStruct((2,) + padded, f32)]
        + [jax.ShapeDtypeStruct((2 * mloc * wide, LANES), bf16)] * half,
        in_specs=[VMEM] * 2,
        out_specs=[VMEM] * (half + 1),
        compiler_params=PARAMS,
        name="edges",
    )(swap(view), ours)
    blocks = pl.pallas_call(
        functools.partial(blocks_kernel, mloc, width, step),
        out_shape=[jax.ShapeDtypeStruct((planes, 2 * mloc * width, LANES), bf16)] * half,
        in_specs=[VMEM],
        out_specs=[VMEM] * half,
        compiler_params=PARAMS,
        cost_estimate=pl.CostEstimate(flops=1 << 24, bytes_accessed=1 << 24, transcendentals=0),
        name="blocks",
    )(both)
    got = [None] * half
    for q in list(range(1, half)) + [0]:
        got[q] = permute(edges[q], members, tiles, functools.partial(beside, q, members, tiles))
    blocks = [blocks[0]] + [
        permute(blocks[q], members, tiles, lambda m, t: (m ^ (2 * q), t)) for q in range(1, half)
    ]
    got = pl.pallas_call(
        join_kernel,
        out_shape=jax.ShapeDtypeStruct((total * wide, LANES), bf16),
        in_specs=[VMEM] * half,
        out_specs=VMEM,
        compiler_params=PARAMS,
        name="join",
    )(*got)
    other = swap(got)
    out_shape = jax.ShapeDtypeStruct((planes, 26, step * LANES), f32)
    part_shape = jax.ShapeDtypeStruct((total // 8, 4, step, 8, LANES), f32)
    out, part = pl.pallas_call(
        functools.partial(inner_kernel, width, step, total),
        out_shape=[out_shape, part_shape],
        in_specs=[VMEM] * half,
        out_specs=[ANY, VMEM],
        scratch_shapes=[
            pltpu.VMEM((planes, total * width, LANES), f32),
            pltpu.VMEM((planes - 2, 26, step * LANES), f32),
            pltpu.SemaphoreType.DMA,
        ],
        compiler_params=PARAMS,
        name="inner",
    )(*blocks)
    out = pl.pallas_call(
        functools.partial(outer_kernel, wide, step, total),
        out_shape=out_shape,
        in_specs=[VMEM, VMEM, VMEM, ANY],
        out_specs=ANY,
        scratch_shapes=[
            pltpu.VMEM((2, total * wide, LANES), f32),
            pltpu.VMEM((2, 26, step * LANES), f32),
            pltpu.SemaphoreType.DMA((2,)),
        ],
        input_output_aliases={3: 0},
        compiler_params=PARAMS,
        name="outer",
    )(got, other, part, out)
    return out.transpose(1, 0, 2)


def solution(mesh):
    sizes = dict(mesh.shape)
    in_specs = (P("member", "tile", None),)
    out_specs = P(None, "tile", "member")
    body = functools.partial(local, sizes["member"], sizes["tile"])
    return jax.shard_map(body, mesh=mesh, in_specs=in_specs, out_specs=out_specs, check_vma=False)
```

time: 68 us -> 13.3 us (0.20)
  waiting for transfers between devices: 31.3 us -> 4.91 us
  between operations: 13.7 us -> 0.04 us
  local copies, waits for them, and re-layouts: 10.1 us -> 0.91 us
  other arithmetic: 6.53 us -> 0 us
  Pallas kernels: 0 us -> 2.37 us
  starting transfers between devices: 6.17 us -> 4.91 us
    reduce_scatter x1 -> x0, waiting for transfers between devices: 27 us -> none  [local(): lax.psum_scatter(flat_tallies.astype(jnp.bfloat16), 'member', scatter_dim...]
    another operation x27 -> x0, local copies, waits for them, and re-layouts: 10 us -> none  [direction_counts(): return jnp.stack(tallies)]
    pallas_call x0 -> x6, Pallas kernels: none -> 2.37 us  [the longest x1 1.27 us: local(): pl.pallas_call(functools.partial(inner_kernel, width, step, total), out_s...]
    or x5 -> x0, other arithmetic: 2.07 us -> none  [the longest x4 2.06 us: direction_counts(): claimed = claimed | chosen]
    div x1 -> x0, other arithmetic: 1.83 us -> none  [local(): return summed / total_members]
    ppermute x2 -> x5, starting transfers between devices: 6.16 us -> 4.91 us  [permute(): return lax.ppermute(value, ('member', 'tile'), pairs)]
    convert_element_type x1 -> x0, other arithmetic: 0.96 us -> none  [local(): shaped.astype(jnp.bfloat16)]
    unnamed x0 -> x2, local copies, waits for them, and re-layouts: none -> 0.91 us
  transfers between devices with their start and end apart: 3 -> 5, of which waited for: 3 -> 3; matrix products, arithmetic and copies ran while one was open for 0% -> 0% of each run, Pallas kernels for 0% -> 10%
where the time goes in v2:
time: 13.3 us; the launch traced here: 13.1 us
  starting transfers between devices  4.91 us (37%)
  waiting for transfers between devices  4.91 us (37%)
  Pallas kernels  2.37 us (18%)
  local copies, waits for them, and re-layouts  0.91 us (7%)
    ppermute x5, waiting for transfers between devices, permute(): return lax.ppermute(value, ('member', 'tile'), pairs)  4.91 us
    ppermute x5, starting transfers between devices, permute(): return lax.ppermute(value, ('member', 'tile'), pairs)  4.91 us
    pallas_call x1, Pallas kernels, local(): pl.pallas_call(functools.partial(inner_kernel, width, step, total), out_s...  1.27 us
    pallas_call x1, Pallas kernels, local(): pl.pallas_call(functools.partial(outer_kernel, wide, step, total), out_sh...  0.99 us
    unnamed x2, local copies, waits for them, and re-layouts  0.91 us
  transfers between devices with their start and end apart: 5, of which 3 were waited for; matrix products, arithmetic and copies ran while one was open for 0% of the time, Pallas kernels for 10%

profile of v2, /device:TPU:0, one launch (start us, length us, event | category | flops | bytes accessed | tf_op | source)
XLA Modules:
  0.0 13.1 jit_solution(16282434945335267669)
XLA Ops:
  0.0 0.5 %collective-permute-start = (f32[6,48,128]{2,1,0:T(8,128)}, f32[6,48,128]{2,1,0:T(8,128)S(1)}, u32[]{:S(2)}, u32[]{:S(2)}) collective-permute-start(f32[6,48,128]{2,1,0:T(8,128)} %bitcast.6), channel_id=1, source_target_pairs={{0,8},{1,9},{2,10},{3,11},{4,12},{5,13},{6,14},{7,15},{8,0},{9,1},... | collective-permute-start | bytes 442376 | tf_op jit(solution)/shard_map/ppermute | solution.py:27
  0.5 0.0 copy-start
  0.5 0.9 %copy-done = f32[2,6,3072]{2,0,1:T(2,128)S(1)} copy-done((f32[2,6,3072]{2,0,1:T(2,128)S(1)}, f32[2,6,3072]{2,0,1:T(2,128)}, u32[]{:S(2)}) %copy-start) | copy-done | bytes 147480
  1.4 0.3 %collective-permute-done.theirs = f32[6,48,128]{2,1,0:T(8,128)S(1)} collective-permute-done((f32[6,48,128]{2,1,0:T(8,128)}, f32[6,48,128]{2,1,0:T(8,128)S(1)}, u32[]{:S(2)}, u32[]{:S(2)}) %collective-permute-start) | collective-permute-done | bytes 147488 | tf_op jit(solution)/shard_map/ppermute | solution.py:27
  1.8 2.9 %collective-permute-start.4 = (bf16[6,40,128]{2,1,0:T(8,128)(2,1)S(1)}, bf16[6,40,128]{2,1,0:T(8,128)(2,1)S(1)}, u32[]{:S(2)}, u32[]{:S(2)}) collective-permute-start(bf16[6,40,128]{2,1,0:T(8,128)(2,1)S(1)} %get-tuple-element.16), channel_id=1, source_target_pairs={{0,16},{1,17},{2,18},{3,19},{4,20},{5,21},{6,22},{7,23},{8,24},{9,... | collective-permute-start | bytes 184328 | tf_op jit(solution)/shard_map/ppermute | solution.py:27
  4.7 1.5 %collective-permute-start.1 = (bf16[64,128]{1,0:T(8,128)(2,1)S(1)}, bf16[64,128]{1,0:T(8,128)(2,1)S(1)}, u32[]{:S(2)}, u32[]{:S(2)}) collective-permute-start(bf16[64,128]{1,0:T(8,128)(2,1)S(1)} %get-tuple-element.12), channel_id=1, source_target_pairs={{0,1},{1,0},{2,3},{3,2},{4,5},{5,4},{6,7},{7,6},{8,24},{9,10},{10,... | collective-permute-start | bytes 49160 | tf_op jit(solution)/shard_map/ppermute | solution.py:27
  6.2 0.0 collective-permute-start.2
  6.2 2.2 %collective-permute-done.1.refs_0_ = bf16[64,128]{1,0:T(8,128)(2,1)S(1)} collective-permute-done((bf16[64,128]{1,0:T(8,128)(2,1)S(1)}, bf16[64,128]{1,0:T(8,128)(2,1)S(1)}, u32[]{:S(2)}, u32[]{:S(2)}) %collective-permute-start.1) | collective-permute-done | bytes 16416 | tf_op jit(solution)/shard_map/ppermute | solution.py:27
  8.4 2.4 %collective-permute-done.2.refs_1_ = bf16[64,128]{1,0:T(8,128)(2,1)S(1)} collective-permute-done((bf16[64,128]{1,0:T(8,128)(2,1)S(1)}, bf16[64,128]{1,0:T(8,128)(2,1)S(1)}, u32[]{:S(2)}, u32[]{:S(2)}) %collective-permute-start.2) | collective-permute-done | bytes 16416 | tf_op jit(solution)/shard_map/ppermute | solution.py:27
  10.9 0.0 collective-permute-start.3
  10.9 0.0 collective-permute-done.4.refs_1_
  10.9 1.3 %inner.1 = (f32[6,26,768]{2,1,0:T(8,128)}, f32[1,4,6,8,128]{4,3,2,1,0:T(8,128)S(1)}) custom-call(bf16[6,40,128]{2,1,0:T(8,128)(2,1)S(1)} %get-tuple-element.15.refs_0_, bf16[6,40,128]{2,1,0:T(8,128)(2,1)S(1)} %collective-permute-done.4.refs_1_), custom_call_target="tpu_custom_call" | custom-call | tf_op jit(solution)/shard_map/inner/pallas_call | solution.py:247
  12.1 0.0 collective-permute-done.3.other
  12.2 1.0 %outer.1 = f32[6,26,768]{2,1,0:T(8,128)} custom-call(bf16[128,128]{1,0:T(8,128)(2,1)S(1)} %join.1.got, bf16[128,128]{1,0:T(8,128)(2,1)S(1)} %collective-permute-done.3.other, f32[1,4,6,8,128]{4,3,2,1,0:T(8,128)S(1)} %get-tuple-element.17.part, f32[6,26,768]{2,1,0:T(8,128)} %get-tuple-element.18.partial_out), custom_call_target="tpu_custom_call", output_to_operand_aliasing={{}: (3, {})} | custom-call | tf_op jit(solution)/shard_map/outer/pallas_call | solution.py:260
  (4 shorter events, 0.1 us)
Async XLA Ops:
  0.0 1.7 %collective-permute-start = (f32[6,48,128]{2,1,0:T(8,128)}, f32[6,48,128]{2,1,0:T(8,128)S(1)}, u32[]{:S(2)}, u32[]{:S(2)}) collective-permute-start(f32[6,48,128]{2,1,0:T(8,128)} %bitcast.6), channel_id=1, source_target_pairs={{0,8},{1,9},{2,10},{3,11},{4,12},{5,13},{6,14},{7,15},{8,0},{9,1},... | collective-permute-start | bytes 442376 | tf_op jit(solution)/shard_map/ppermute | solution.py:27
  0.5 0.9 %copy-start = (f32[2,6,3072]{2,0,1:T(2,128)S(1)}, f32[2,6,3072]{2,0,1:T(2,128)}, u32[]{:S(2)}) copy-start(f32[2,6,3072]{2,0,1:T(2,128)} %param.1) | copy-start | bytes 442372
  1.8 9.1 %collective-permute-start.4 = (bf16[6,40,128]{2,1,0:T(8,128)(2,1)S(1)}, bf16[6,40,128]{2,1,0:T(8,128)(2,1)S(1)}, u32[]{:S(2)}, u32[]{:S(2)}) collective-permute-start(bf16[6,40,128]{2,1,0:T(8,128)(2,1)S(1)} %get-tuple-element.16), channel_id=1, source_target_pairs={{0,16},{1,17},{2,18},{3,19},{4,20},{5,21},{6,22},{7,23},{8,24},{9,... | collective-permute-start | bytes 184328 | tf_op jit(solution)/shard_map/ppermute | solution.py:27
  4.7 3.7 %collective-permute-start.1 = (bf16[64,128]{1,0:T(8,128)(2,1)S(1)}, bf16[64,128]{1,0:T(8,128)(2,1)S(1)}, u32[]{:S(2)}, u32[]{:S(2)}) collective-permute-start(bf16[64,128]{1,0:T(8,128)(2,1)S(1)} %get-tuple-element.12), channel_id=1, source_target_pairs={{0,1},{1,0},{2,3},{3,2},{4,5},{5,4},{6,7},{7,6},{8,24},{9,10},{10,... | collective-permute-start | bytes 49160 | tf_op jit(solution)/shard_map/ppermute | solution.py:27
  6.2 4.6 %collective-permute-start.2 = (bf16[64,128]{1,0:T(8,128)(2,1)S(1)}, bf16[64,128]{1,0:T(8,128)(2,1)S(1)}, u32[]{:S(2)}, u32[]{:S(2)}) collective-permute-start(bf16[64,128]{1,0:T(8,128)(2,1)S(1)} %get-tuple-element.13), channel_id=1, source_target_pairs={{0,17},{1,16},{2,19},{3,18},{4,21},{5,20},{6,23},{7,22},{8,24},{9,... | collective-permute-start | bytes 49160 | tf_op jit(solution)/shard_map/ppermute | solution.py:27
  10.9 1.3 %collective-permute-start.3 = (bf16[128,128]{1,0:T(8,128)(2,1)S(1)}, bf16[128,128]{1,0:T(8,128)(2,1)S(1)}, u32[]{:S(2)}, u32[]{:S(2)}) collective-permute-start(bf16[128,128]{1,0:T(8,128)(2,1)S(1)} %join.1.got), channel_id=1, source_target_pairs={{0,8},{1,9},{2,10},{3,11},{4,12},{5,13},{6,14},{7,15},{8,0},{9,1},... | collective-permute-start | bytes 98312 | tf_op jit(solution)/shard_map/ppermute | solution.py:27

commit v3 on v2

--- a/solution.py
+++ b/solution.py
@@ -47,6 +47,16 @@
     out[:, LEAD + rows : LEAD + rows + LEAD, :] = fill
 
 
+def start_kernel(mloc, wide, step, src, ours, *sends):
+    load_kernel(src, ours)
+    pair = lax.axis_index("member") // 2
+    for q, send in enumerate(sends):
+        base = (pair ^ (q + 1)) * (2 * step * mloc) + LEAD - EDGE * mloc
+        for p in range(src.shape[0]):
+            parts = [ours[p, pl.ds(base + i, wide, stride=mloc), :] for i in range(mloc)]
+            send[p] = jnp.concatenate(parts, axis=0).astype(jnp.bfloat16)
+
+
 def spread_kernel(theirs, ours, both):
     core = lax.axis_index("member") % 2
     both[core] = ours[...]
@@ -64,21 +74,32 @@
     pair = lax.axis_index("member") // 2
     plane = (ours.shape[0] - 1) * (1 - edge_side())
     for q, edge in enumerate(edges):
-        edge[...] = window(both, mloc, plane, (pair ^ q) * (2 * step), wide)
-
-
-def blocks_kernel(mloc, width, step, both, *blocks):
-    me = lax.axis_index("member")
-    for q, block in enumerate(blocks):
-        for p in range(block.shape[0]):
-            block[p] = window(both, mloc, p, (me ^ (2 * q)) * step, width)
+        edge[...] = window(both, mloc, plane, (pair ^ q) * (2 * step), wide).astype(jnp.float32)
+
+
+def block_kernel(mloc, width, step, both, block):
+    start = lax.axis_index("member") * step
+    for p in range(block.shape[0]):
+        block[p] = window(both, mloc, p, start, width)
+
+
+def cross_kernel(mloc, width, wide, step, *refs):
+    n = len(refs) - 3
+    raws, (keep, give, stage) = refs[:n], refs[n:]
+    core = lax.axis_index("member") % 2
+    for q, raw in enumerate(raws):
+        stage[...] = raw[...].astype(jnp.float32)
+        for dest, start in ((keep, core * step), (give, (1 - core) * step)):
+            for p in range(raw.shape[0]):
+                parts = [stage[p, pl.ds(i * wide + start, width), :] for i in range(mloc)]
+                dest[q, p] = jnp.concatenate(parts, axis=0).astype(jnp.bfloat16)
 
 
 def join_kernel(*refs):
     bufs, out = refs[:-1], refs[-1]
     rows = bufs[0].shape[0]
     for k, buf in enumerate(bufs):
-        out[k * rows : (k + 1) * rows, :] = buf[...]
+        out[(len(bufs) - 1 - k) * rows : (len(bufs) - k) * rows, :] = buf[...].astype(out.dtype)
 
 
 def keys_of(stage, p, group, width, step, start):
@@ -135,12 +156,15 @@
         out[at] = out[at] + share[:n] if add else share[:n]
 
 
-def inner_kernel(width, step, total, *refs):
-    blocks, (out, part, stage, tile_out, sem) = refs[:-5], refs[-5:]
-    planes, rows = blocks[0].shape[0], blocks[0].shape[1]
-    for q, block in enumerate(blocks):
-        for p in range(planes):
-            stage[p, q * rows : (q + 1) * rows, :] = block[p].astype(jnp.float32)
+def inner_kernel(width, step, total, block, keep, came, out, part, stage, tile_out, sem):
+    planes, rows = block.shape[0], block.shape[1]
+    first = lax.axis_index("member") % 2 == 0
+    for p in range(planes):
+        stage[p, 0:rows, :] = block[p].astype(jnp.float32)
+        for q in range(keep.shape[0]):
+            here, there = keep[q, p].astype(jnp.float32), came[q, p].astype(jnp.float32)
+            pairs = jnp.where(first, here, there), jnp.where(first, there, here)
+            stage[p, (q + 1) * rows : (q + 2) * rows, :] = jnp.concatenate(pairs, axis=0)
     for group in range(total // 8):
         layers = [keys_of(stage, p, group, width, step, 0) for p in range(planes)]
         for j in range(step):
@@ -201,53 +225,54 @@
     view = fields.reshape(mloc, planes, spread, LANES).transpose(1, 2, 0, 3)
     view = view.reshape(planes, spread * mloc, LANES)
     padded = (planes, spread * mloc + 2 * LEAD, LANES)
-    ours = pl.pallas_call(
-        load_kernel,
-        out_shape=jax.ShapeDtypeStruct(padded, f32),
+    ours, *sends = pl.pallas_call(
+        functools.partial(start_kernel, mloc, wide, step),
+        out_shape=[jax.ShapeDtypeStruct(padded, f32)]
+        + [jax.ShapeDtypeStruct((planes, mloc * wide, LANES), bf16)] * (half - 1),
         in_specs=[VMEM],
-        out_specs=VMEM,
+        out_specs=[VMEM] * half,
         compiler_params=PARAMS,
         name="load",
     )(view)
     both, *edges = pl.pallas_call(
         functools.partial(edges_kernel, mloc, wide, step),
         out_shape=[jax.ShapeDtypeStruct((2,) + padded, f32)]
-        + [jax.ShapeDtypeStruct((2 * mloc * wide, LANES), bf16)] * half,
+        + [jax.ShapeDtypeStruct((2 * mloc * wide, LANES), f32)] * half,
         in_specs=[VMEM] * 2,
         out_specs=[VMEM] * (half + 1),
         compiler_params=PARAMS,
         name="edges",
     )(swap(view), ours)
-    blocks = pl.pallas_call(
-        functools.partial(blocks_kernel, mloc, width, step),
-        out_shape=[jax.ShapeDtypeStruct((planes, 2 * mloc * width, LANES), bf16)] * half,
+    raws = [permute(sends[q - 1], members, tiles, lambda m, t: (m ^ (2 * q), t)) for q in range(1, half)]
+    *raws, both = lax.optimization_barrier((*raws, both))
+    block = pl.pallas_call(
+        functools.partial(block_kernel, mloc, width, step),
+        out_shape=jax.ShapeDtypeStruct((planes, 2 * mloc * width, LANES), bf16),
         in_specs=[VMEM],
-        out_specs=[VMEM] * half,
-        compiler_params=PARAMS,
-        cost_estimate=pl.CostEstimate(flops=1 << 24, bytes_accessed=1 << 24, transcendentals=0),
-        name="blocks",
+        out_specs=VMEM,
+        compiler_params=PARAMS,
+        name="block",
     )(both)
+    kept = jax.ShapeDtypeStruct((half - 1, planes, mloc * width, LANES), bf16)
+    keep, give = pl.pallas_call(
+        functools.partial(cross_kernel, mloc, width, wide, step),
+        out_shape=[kept, kept],
+        in_specs=[VMEM] * (half - 1),
+        out_specs=[VMEM] * 2,
+        scratch_shapes=[pltpu.VMEM((planes, mloc * wide, LANES), f32)],
+        compiler_params=PARAMS,
+        name="cross",
+    )(*raws)
+    came = swap(give)
     got = [None] * half
     for q in list(range(1, half)) + [0]:
         got[q] = permute(edges[q], members, tiles, functools.partial(beside, q, members, tiles))
-    blocks = [blocks[0]] + [
-        permute(blocks[q], members, tiles, lambda m, t: (m ^ (2 * q), t)) for q in range(1, half)
-    ]
-    got = pl.pallas_call(
-        join_kernel,
-        out_shape=jax.ShapeDtypeStruct((total * wide, LANES), bf16),
-        in_specs=[VMEM] * half,
-        out_specs=VMEM,
-        compiler_params=PARAMS,
-        name="join",
-    )(*got)
-    other = swap(got)
     out_shape = jax.ShapeDtypeStruct((planes, 26, step * LANES), f32)
     part_shape = jax.ShapeDtypeStruct((total // 8, 4, step, 8, LANES), f32)
     out, part = pl.pallas_call(
         functools.partial(inner_kernel, width, step, total),
         out_shape=[out_shape, part_shape],
-        in_specs=[VMEM] * half,
+        in_specs=[VMEM] * 3,
         out_specs=[ANY, VMEM],
         scratch_shapes=[
             pltpu.VMEM((planes, total * width, LANES), f32),
@@ -256,7 +281,18 @@
         ],
         compiler_params=PARAMS,
         name="inner",
-    )(*blocks)
+    )(block, keep, came)
+    *got, part = lax.optimization_barrier((*got[::-1], part))
+    got = got[::-1]
+    got = pl.pallas_call(
+        join_kernel,
+        out_shape=jax.ShapeDtypeStruct((total * wide, LANES), bf16),
+        in_specs=[VMEM] * half,
+        out_specs=VMEM,
+        compiler_params=PARAMS,
+        name="join",
+    )(*got[::-1])
+    other = swap(got)
     out = pl.pallas_call(
         functools.partial(outer_kernel, wide, step, total),
         out_shape=out_shape,

time: 13.3 us -> 11.8 us (0.89)
  waiting for transfers between devices: 4.91 us -> 3.16 us
  starting transfers between devices: 4.91 us -> 5.18 us
    ppermute x5 -> x6, waiting for transfers between devices: 4.91 us -> 3.16 us  [permute(): return lax.ppermute(value, ('member', 'tile'), pairs)]
    ppermute x5 -> x6, starting transfers between devices: 4.91 us -> 5.18 us  [permute(): return lax.ppermute(value, ('member', 'tile'), pairs)]
  transfers between devices with their start and end apart: 5 -> 6, of which waited for: 3 -> 4; matrix products, arithmetic and copies ran while one was open for 0% -> 0% of each run, Pallas kernels for 10% -> 12%
where the time goes in v3:
time: 11.8 us; the launch traced here: 11.7 us
  starting transfers between devices  5.18 us (44%)
  waiting for transfers between devices  3.16 us (27%)
  Pallas kernels  2.38 us (20%)
  local copies, waits for them, and re-layouts  0.91 us (8%)
    ppermute x6, starting transfers between devices, permute(): return lax.ppermute(value, ('member', 'tile'), pairs)  5.18 us
    ppermute x6, waiting for transfers between devices, permute(): return lax.ppermute(value, ('member', 'tile'), pairs)  3.16 us
    pallas_call x1, Pallas kernels, local(): pl.pallas_call(functools.partial(inner_kernel, width, step, total), out_s...  1.28 us
    pallas_call x1, Pallas kernels, local(): pl.pallas_call(functools.partial(outer_kernel, wide, step, total), out_sh...  0.97 us
    unnamed x2, local copies, waits for them, and re-layouts  0.91 us
  transfers between devices with their start and end apart: 6, of which 4 were waited for; matrix products, arithmetic and copies ran while one was open for 0% of the time, Pallas kernels for 12%

profile of v3, /device:TPU:0, one launch (start us, length us, event | category | flops | bytes accessed | tf_op | source)
XLA Modules:
  0.0 11.7 jit_solution(7366105189188201911)
XLA Ops:
  0.0 0.5 %collective-permute-start = (f32[6,48,128]{2,1,0:T(8,128)}, f32[6,48,128]{2,1,0:T(8,128)S(1)}, u32[]{:S(2)}, u32[]{:S(2)}) collective-permute-start(f32[6,48,128]{2,1,0:T(8,128)} %bitcast.6), channel_id=1, source_target_pairs={{0,8},{1,9},{2,10},{3,11},{4,12},{5,13},{6,14},{7,15},{8,0},{9,1},... | collective-permute-start | bytes 442376 | tf_op jit(solution)/shard_map/ppermute | solution.py:27
  0.5 0.0 copy-start
  0.5 0.9 %copy-done = f32[2,6,3072]{2,0,1:T(2,128)S(1)} copy-done((f32[2,6,3072]{2,0,1:T(2,128)S(1)}, f32[2,6,3072]{2,0,1:T(2,128)}, u32[]{:S(2)}) %copy-start) | copy-done | bytes 147480
  1.4 2.6 %collective-permute-start.3 = (bf16[6,32,128]{2,1,0:T(8,128)(2,1)S(1)}, bf16[6,32,128]{2,1,0:T(8,128)(2,1)S(1)}, u32[]{:S(2)}, u32[]{:S(2)}) collective-permute-start(bf16[6,32,128]{2,1,0:T(8,128)(2,1)S(1)} %get-tuple-element.22), channel_id=1, source_target_pairs={{0,16},{1,17},{2,18},{3,19},{4,20},{5,21},{6,22},{7,23},{8,24},{9,... | collective-permute-start | bytes 147464 | tf_op jit(solution)/shard_map/ppermute | solution.py:27
  3.9 0.0 collective-permute-done.theirs
  4.0 0.1 edges.1
  4.0 1.6 %collective-permute-start.1 = (f32[64,128]{1,0:T(8,128)S(1)}, f32[64,128]{1,0:T(8,128)S(1)}, u32[]{:S(2)}, u32[]{:S(2)}) collective-permute-start(f32[64,128]{1,0:T(8,128)S(1)} %get-tuple-element.20), channel_id=1, source_target_pairs={{0,17},{1,16},{2,19},{3,18},{4,21},{5,20},{6,23},{7,22},{8,24},{9,... | collective-permute-start | bytes 98312 | tf_op jit(solution)/shard_map/ppermute | solution.py:27
  5.6 0.5 %collective-permute-start.2 = (f32[64,128]{1,0:T(8,128)S(1)}, f32[64,128]{1,0:T(8,128)S(1)}, u32[]{:S(2)}, u32[]{:S(2)}) collective-permute-start(f32[64,128]{1,0:T(8,128)S(1)} %get-tuple-element.21), channel_id=1, source_target_pairs={{0,1},{1,0},{2,3},{3,2},{4,5},{5,4},{6,7},{7,6},{8,24},{9,10},{10,... | collective-permute-start | bytes 98312 | tf_op jit(solution)/shard_map/ppermute | solution.py:27
  6.1 0.3 %collective-permute-done.3.refs_0_ = bf16[6,32,128]{2,1,0:T(8,128)(2,1)S(1)} collective-permute-done((bf16[6,32,128]{2,1,0:T(8,128)(2,1)S(1)}, bf16[6,32,128]{2,1,0:T(8,128)(2,1)S(1)}, u32[]{:S(2)}, u32[]{:S(2)}) %collective-permute-start.3) | collective-permute-done | bytes 49184 | tf_op jit(solution)/shard_map/ppermute | solution.py:27
  6.4 0.1 collective-permute-start.4
  6.5 1.2 %collective-permute-done.4.came = bf16[1,6,20,128]{3,2,1,0:T(8,128)(2,1)S(1)} collective-permute-done((bf16[1,6,20,128]{3,2,1,0:T(8,128)(2,1)S(1)}, bf16[1,6,20,128]{3,2,1,0:T(8,128)(2,1)S(1)}, u32[]{:S(2)}, u32[]{:S(2)}) %collective-permute-start.4) | collective-permute-done | bytes 30752 | tf_op jit(solution)/shard_map/ppermute | solution.py:27
  7.7 1.3 %inner.1 = (f32[6,26,768]{2,1,0:T(8,128)}, f32[1,4,6,8,128]{4,3,2,1,0:T(8,128)S(1)}) custom-call(bf16[6,40,128]{2,1,0:T(8,128)(2,1)S(1)} %block.1, bf16[1,6,20,128]{3,2,1,0:T(8,128)(2,1)S(1)} %get-tuple-element.26.keep, bf16[1,6,20,128]{3,2,1,0:T(8,128)(2,1)S(1)} %collective-permute-done.4.came), custom_call_target="tpu_custom_call" | custom-call | tf_op jit(solution)/shard_map/inner/pallas_call | solution.py:272
  9.0 0.0 collective-permute-done.1.refs_0_
  9.0 0.5 %collective-permute-done.2.refs_1_ = f32[64,128]{1,0:T(8,128)S(1)} collective-permute-done((f32[64,128]{1,0:T(8,128)S(1)}, f32[64,128]{1,0:T(8,128)S(1)}, u32[]{:S(2)}, u32[]{:S(2)}) %collective-permute-start.2) | collective-permute-done | bytes 32800 | tf_op jit(solution)/shard_map/ppermute | solution.py:27
  9.5 0.0 collective-permute-start.5
  9.5 1.2 %collective-permute-done.5.other = bf16[128,128]{1,0:T(8,128)(2,1)S(1)} collective-permute-done((bf16[128,128]{1,0:T(8,128)(2,1)S(1)}, bf16[128,128]{1,0:T(8,128)(2,1)S(1)}, u32[]{:S(2)}, u32[]{:S(2)}) %collective-permute-start.5) | collective-permute-done | bytes 32800 | tf_op jit(solution)/shard_map/ppermute | solution.py:27
  10.7 1.0 %outer.1 = f32[6,26,768]{2,1,0:T(8,128)} custom-call(bf16[128,128]{1,0:T(8,128)(2,1)S(1)} %join.1.got, bf16[128,128]{1,0:T(8,128)(2,1)S(1)} %collective-permute-done.5.other, f32[1,4,6,8,128]{4,3,2,1,0:T(8,128)S(1)} %get-tuple-element.31.part, f32[6,26,768]{2,1,0:T(8,128)} %get-tuple-element.32.partial_out), custom_call_target="tpu_custom_call", output_to_operand_aliasing={{}: (3, {})} | custom-call | tf_op jit(solution)/shard_map/outer/pallas_call | solution.py:296
  (4 shorter events, 0.1 us)
Async XLA Ops:
  0.0 3.9 %collective-permute-start = (f32[6,48,128]{2,1,0:T(8,128)}, f32[6,48,128]{2,1,0:T(8,128)S(1)}, u32[]{:S(2)}, u32[]{:S(2)}) collective-permute-start(f32[6,48,128]{2,1,0:T(8,128)} %bitcast.6), channel_id=1, source_target_pairs={{0,8},{1,9},{2,10},{3,11},{4,12},{5,13},{6,14},{7,15},{8,0},{9,1},... | collective-permute-start | bytes 442376 | tf_op jit(solution)/shard_map/ppermute | solution.py:27
  0.5 0.9 %copy-start = (f32[2,6,3072]{2,0,1:T(2,128)S(1)}, f32[2,6,3072]{2,0,1:T(2,128)}, u32[]{:S(2)}) copy-start(f32[2,6,3072]{2,0,1:T(2,128)} %param.1) | copy-start | bytes 442372
  1.4 5.0 %collective-permute-start.3 = (bf16[6,32,128]{2,1,0:T(8,128)(2,1)S(1)}, bf16[6,32,128]{2,1,0:T(8,128)(2,1)S(1)}, u32[]{:S(2)}, u32[]{:S(2)}) collective-permute-start(bf16[6,32,128]{2,1,0:T(8,128)(2,1)S(1)} %get-tuple-element.22), channel_id=1, source_target_pairs={{0,16},{1,17},{2,18},{3,19},{4,20},{5,21},{6,22},{7,23},{8,24},{9,... | collective-permute-start | bytes 147464 | tf_op jit(solution)/shard_map/ppermute | solution.py:27
  4.0 5.0 %collective-permute-start.1 = (f32[64,128]{1,0:T(8,128)S(1)}, f32[64,128]{1,0:T(8,128)S(1)}, u32[]{:S(2)}, u32[]{:S(2)}) collective-permute-start(f32[64,128]{1,0:T(8,128)S(1)} %get-tuple-element.20), channel_id=1, source_target_pairs={{0,17},{1,16},{2,19},{3,18},{4,21},{5,20},{6,23},{7,22},{8,24},{9,... | collective-permute-start | bytes 98312 | tf_op jit(solution)/shard_map/ppermute | solution.py:27
  5.6 3.9 %collective-permute-start.2 = (f32[64,128]{1,0:T(8,128)S(1)}, f32[64,128]{1,0:T(8,128)S(1)}, u32[]{:S(2)}, u32[]{:S(2)}) collective-permute-start(f32[64,128]{1,0:T(8,128)S(1)} %get-tuple-element.21), channel_id=1, source_target_pairs={{0,1},{1,0},{2,3},{3,2},{4,5},{5,4},{6,7},{7,6},{8,24},{9,10},{10,... | collective-permute-start | bytes 98312 | tf_op jit(solution)/shard_map/ppermute | solution.py:27
  6.4 1.3 %collective-permute-start.4 = (bf16[1,6,20,128]{3,2,1,0:T(8,128)(2,1)S(1)}, bf16[1,6,20,128]{3,2,1,0:T(8,128)(2,1)S(1)}, u32[]{:S(2)}, u32[]{:S(2)}) collective-permute-start(bf16[1,6,20,128]{3,2,1,0:T(8,128)(2,1)S(1)} %get-tuple-element.27), channel_id=1, source_target_pairs={{0,8},{1,9},{2,10},{3,11},{4,12},{5,13},{6,14},{7,15},{8,0},{9,1},... | collective-permute-start | bytes 92168 | tf_op jit(solution)/shard_map/ppermute | solution.py:27
  9.5 1.2 %collective-permute-start.5 = (bf16[128,128]{1,0:T(8,128)(2,1)S(1)}, bf16[128,128]{1,0:T(8,128)(2,1)S(1)}, u32[]{:S(2)}, u32[]{:S(2)}) collective-permute-start(bf16[128,128]{1,0:T(8,128)(2,1)S(1)} %join.1.got), channel_id=1, source_target_pairs={{0,8},{1,9},{2,10},{3,11},{4,12},{5,13},{6,14},{7,15},{8,0},{9,1},... | collective-permute-start | bytes 98312 | tf_op jit(solution)/shard_map/ppermute | solution.py:27

commit v4 on v3

--- a/solution.py
+++ b/solution.py
@@ -28,15 +28,14 @@
 
 
 def beside(q, members, tiles, m, t):
-    if m % 2 == 0:
-        return m ^ (2 * q), t ^ 1
-    if t == 0 or t == tiles - 1:
+    up = m % 2 == 0
+    if t == (tiles - 1 if up else 0):
         return m ^ (2 * q if q else members // 2), t
-    return m ^ (2 * q), (t + 1 if t % 2 else t - 1)
+    return m ^ (2 * q + 1), (t + 1 if up else t - 1)
 
 
 def edge_side():
-    return (lax.axis_index("member") + lax.axis_index("tile")) % 2
+    return lax.axis_index("member") % 2
 
 
 def load_kernel(src, out):
@@ -74,7 +73,7 @@
     pair = lax.axis_index("member") // 2
     plane = (ours.shape[0] - 1) * (1 - edge_side())
     for q, edge in enumerate(edges):
-        edge[...] = window(both, mloc, plane, (pair ^ q) * (2 * step), wide).astype(jnp.float32)
+        edge[...] = window(both, mloc, plane, (pair ^ q) * (2 * step), wide)
 
 
 def block_kernel(mloc, width, step, both, block):
@@ -84,22 +83,23 @@
 
 
 def cross_kernel(mloc, width, wide, step, *refs):
-    n = len(refs) - 3
-    raws, (keep, give, stage) = refs[:n], refs[n:]
+    n = len(refs) - 2 * mloc - 1
+    raws, keeps, gives, stage = refs[:n], refs[n : n + mloc], refs[n + mloc : -1], refs[-1]
     core = lax.axis_index("member") % 2
     for q, raw in enumerate(raws):
+        planes = raw.shape[0]
         stage[...] = raw[...].astype(jnp.float32)
-        for dest, start in ((keep, core * step), (give, (1 - core) * step)):
-            for p in range(raw.shape[0]):
-                parts = [stage[p, pl.ds(i * wide + start, width), :] for i in range(mloc)]
-                dest[q, p] = jnp.concatenate(parts, axis=0).astype(jnp.bfloat16)
+        for dests, start in ((keeps, core * step), (gives, (1 - core) * step)):
+            for i, dest in enumerate(dests):
+                parts = [stage[p, pl.ds(i * wide + start, width), :] for p in range(planes)]
+                dest[q] = jnp.concatenate(parts, axis=0).astype(jnp.bfloat16)
 
 
 def join_kernel(*refs):
     bufs, out = refs[:-1], refs[-1]
     rows = bufs[0].shape[0]
     for k, buf in enumerate(bufs):
-        out[(len(bufs) - 1 - k) * rows : (len(bufs) - k) * rows, :] = buf[...].astype(out.dtype)
+        out[(len(bufs) - 1 - k) * rows : (len(bufs) - k) * rows, :] = buf[...]
 
 
 def keys_of(stage, p, group, width, step, start):
@@ -108,7 +108,7 @@
     at64, at63 = lane == 64, lane == 63
     base = group * 8 * width + start
     value = {
-        j: stage[p, pl.ds(base + j, 8, stride=width), :] * 32.0
+        j: (stage if p is None else stage.at[p])[pl.ds(base + j, 8, stride=width), :] * 32.0
         for j in range(EDGE - 2, EDGE + step + 2)
     }
     keys = {}
@@ -156,57 +156,64 @@
         out[at] = out[at] + share[:n] if add else share[:n]
 
 
-def inner_kernel(width, step, total, block, keep, came, out, part, stage, tile_out, sem):
+def inner_kernel(mloc, width, step, total, block, *refs):
+    keeps, cames, (tile_out, part, stage) = refs[:mloc], refs[mloc : 2 * mloc], refs[2 * mloc :]
     planes, rows = block.shape[0], block.shape[1]
-    first = lax.axis_index("member") % 2 == 0
+    first = lax.axis_index("member") % 2 == 1
     for p in range(planes):
         stage[p, 0:rows, :] = block[p].astype(jnp.float32)
-        for q in range(keep.shape[0]):
-            here, there = keep[q, p].astype(jnp.float32), came[q, p].astype(jnp.float32)
-            pairs = jnp.where(first, here, there), jnp.where(first, there, here)
-            stage[p, (q + 1) * rows : (q + 2) * rows, :] = jnp.concatenate(pairs, axis=0)
+    for q in range(keeps[0].shape[0]):
+        here = [keep[q].astype(jnp.float32) for keep in keeps]
+        there = [came[q].astype(jnp.float32) for came in cames]
+        both = [jnp.where(first, a, b) for a, b in zip(here, there)]
+        both += [jnp.where(first, b, a) for a, b in zip(here, there)]
+        for p in range(planes):
+            parts = [value[p * width : (p + 1) * width] for value in both]
+            stage[p, (q + 1) * rows : (q + 2) * rows, :] = jnp.concatenate(parts, axis=0)
     for group in range(total // 8):
-        layers = [keys_of(stage, p, group, width, step, 0) for p in range(planes)]
+        layers = []
+        for p in range(planes):
+            layers.append(keys_of(stage, p, group, width, step, 0))
+            if p == 1:
+                for j in range(step):
+                    part[group, 0, j] = jnp.minimum(layers[0][0][j] + 9.0, layers[1][0][j] + 18.0)
+                    part[group, 1, j] = layers[0][1][j]
+            if p < 2:
+                continue
+            for j in range(step):
+                best = jnp.minimum(layers[p - 2][0][j], layers[p - 1][0][j] + 9.0)
+                best = jnp.minimum(best, layers[p][0][j] + 18.0)
+                tally(best, layers[p - 1][1][j], tile_out, p - 2, j, group > 0, total)
         for j in range(step):
-            key = [layer[0][j] for layer in layers]
-            value = [layer[1][j] for layer in layers]
-            part[group, 0, j] = jnp.minimum(key[0] + 9.0, key[1] + 18.0)
-            part[group, 1, j] = value[0]
-            part[group, 2, j] = jnp.minimum(key[planes - 2], key[planes - 1] + 9.0)
-            part[group, 3, j] = value[planes - 1]
-            for p in range(1, planes - 1):
-                best = jnp.minimum(jnp.minimum(key[p - 1], key[p] + 9.0), key[p + 1] + 18.0)
-                tally(best, value[p], tile_out, p - 1, j, group > 0, total)
-    copy = pltpu.make_async_copy(tile_out, out.at[pl.ds(1, planes - 2)], sem)
-    copy.start()
-    copy.wait()
-
-
-def outer_kernel(wide, step, total, got, other, part, partial_out, out, stage, tile_out, sem):
+            part[group, 2, j] = jnp.minimum(layers[-2][0][j], layers[-1][0][j] + 9.0)
+            part[group, 3, j] = layers[-1][1][j]
+
+
+def half_kernel(wide, step, total, other, halo, part, source, out, stage, tile_out, sem):
     planes = out.shape[0]
     tile, tiles = lax.axis_index("tile"), lax.axis_size("tile")
-    side = edge_side()
+    end = edge_side() if other else 1 - edge_side()
     start = (lax.axis_index("member") % 2) * step
-    stage[1 - side] = got[...].astype(jnp.float32)
-    stage[side] = other[...].astype(jnp.float32)
-
-    @pl.when(tile == 0)
+    bias = end.astype(jnp.float32) * 18.0
+    copies = []
+    if not other:
+        copies.append(pltpu.make_async_copy(source, out.at[pl.ds(1, planes - 2)], sem.at[0]))
+        copies[0].start()
+    stage[...] = halo[...].astype(jnp.float32)
+
+    @pl.when(tile == end * (tiles - 1))
     def _():
-        stage[0] = jnp.full(stage.shape[1:], PAD, jnp.float32)
-
-    @pl.when(tile == tiles - 1)
-    def _():
-        stage[1] = jnp.full(stage.shape[1:], PAD, jnp.float32)
-
-    for end, (plane, bias) in enumerate(((0, 0.0), (planes - 1, 18.0))):
-        for group in range(total // 8):
-            keys, _ = keys_of(stage, end, group, wide, step, start)
-            for j in range(step):
-                best = jnp.minimum(part[group, 2 * end, j], keys[j] + bias)
-                tally(best, part[group, 2 * end + 1, j], tile_out, end, j, group > 0, total)
-        pltpu.make_async_copy(tile_out.at[end], out.at[plane], sem.at[end]).start()
-    for end, plane in enumerate((0, planes - 1)):
-        pltpu.make_async_copy(tile_out.at[end], out.at[plane], sem.at[end]).wait()
+        stage[...] = jnp.full(stage.shape, PAD, jnp.float32)
+
+    for group in range(total // 8):
+        keys, _ = keys_of(stage, None, group, wide, step, start)
+        for j in range(step):
+            best = jnp.minimum(part[group, 2 * end, j], keys[j] + bias)
+            tally(best, part[group, 2 * end + 1, j], tile_out, 0, j, group > 0, total)
+    copies.append(pltpu.make_async_copy(tile_out.at[0], out.at[end * (planes - 1)], sem.at[1]))
+    copies[-1].start()
+    for copy in copies:
+        copy.wait()
 
 
 def local(members, tiles, fields):
@@ -237,13 +244,13 @@
     both, *edges = pl.pallas_call(
         functools.partial(edges_kernel, mloc, wide, step),
         out_shape=[jax.ShapeDtypeStruct((2,) + padded, f32)]
-        + [jax.ShapeDtypeStruct((2 * mloc * wide, LANES), f32)] * half,
+        + [jax.ShapeDtypeStruct((2 * mloc * wide, LANES), bf16)] * half,
         in_specs=[VMEM] * 2,
         out_specs=[VMEM] * (half + 1),
         compiler_params=PARAMS,
         name="edges",
     )(swap(view), ours)
-    raws = [permute(sends[q - 1], members, tiles, lambda m, t: (m ^ (2 * q), t)) for q in range(1, half)]
+    raws = [permute(sends[q - 1], members, tiles, lambda m, t: (m ^ (2 * q + 1), t)) for q in range(1, half)]
     *raws, both = lax.optimization_barrier((*raws, both))
     block = pl.pallas_call(
         functools.partial(block_kernel, mloc, width, step),
@@ -253,35 +260,31 @@
         compiler_params=PARAMS,
         name="block",
     )(both)
-    kept = jax.ShapeDtypeStruct((half - 1, planes, mloc * width, LANES), bf16)
-    keep, give = pl.pallas_call(
+    kept = jax.ShapeDtypeStruct((half - 1, planes * width, LANES), bf16)
+    crossed = pl.pallas_call(
         functools.partial(cross_kernel, mloc, width, wide, step),
-        out_shape=[kept, kept],
+        out_shape=[kept] * (2 * mloc),
         in_specs=[VMEM] * (half - 1),
-        out_specs=[VMEM] * 2,
+        out_specs=[VMEM] * (2 * mloc),
         scratch_shapes=[pltpu.VMEM((planes, mloc * wide, LANES), f32)],
         compiler_params=PARAMS,
         name="cross",
     )(*raws)
-    came = swap(give)
+    keeps, cames = crossed[:mloc], [swap(give) for give in crossed[mloc:]]
     got = [None] * half
     for q in list(range(1, half)) + [0]:
         got[q] = permute(edges[q], members, tiles, functools.partial(beside, q, members, tiles))
     out_shape = jax.ShapeDtypeStruct((planes, 26, step * LANES), f32)
     part_shape = jax.ShapeDtypeStruct((total // 8, 4, step, 8, LANES), f32)
-    out, part = pl.pallas_call(
-        functools.partial(inner_kernel, width, step, total),
-        out_shape=[out_shape, part_shape],
-        in_specs=[VMEM] * 3,
-        out_specs=[ANY, VMEM],
-        scratch_shapes=[
-            pltpu.VMEM((planes, total * width, LANES), f32),
-            pltpu.VMEM((planes - 2, 26, step * LANES), f32),
-            pltpu.SemaphoreType.DMA,
-        ],
+    inner, part = pl.pallas_call(
+        functools.partial(inner_kernel, mloc, width, step, total),
+        out_shape=[jax.ShapeDtypeStruct((planes - 2, 26, step * LANES), f32), part_shape],
+        in_specs=[VMEM] * (1 + 2 * mloc),
+        out_specs=[VMEM, VMEM],
+        scratch_shapes=[pltpu.VMEM((planes, total * width, LANES), f32)],
         compiler_params=PARAMS,
         name="inner",
-    )(block, keep, came)
+    )(block, *keeps, *cames)
     *got, part = lax.optimization_barrier((*got[::-1], part))
     got = got[::-1]
     got = pl.pallas_call(
@@ -293,20 +296,22 @@
         name="join",
     )(*got[::-1])
     other = swap(got)
-    out = pl.pallas_call(
-        functools.partial(outer_kernel, wide, step, total),
-        out_shape=out_shape,
-        in_specs=[VMEM, VMEM, VMEM, ANY],
-        out_specs=ANY,
-        scratch_shapes=[
-            pltpu.VMEM((2, total * wide, LANES), f32),
-            pltpu.VMEM((2, 26, step * LANES), f32),
-            pltpu.SemaphoreType.DMA((2,)),
-        ],
-        input_output_aliases={3: 0},
-        compiler_params=PARAMS,
-        name="outer",
-    )(got, other, part, out)
+    out = inner
+    for other, halo in enumerate((got, other)):
+        out = pl.pallas_call(
+            functools.partial(half_kernel, wide, step, total, other),
+            out_shape=out_shape,
+            in_specs=[VMEM, VMEM, ANY if other else VMEM],
+            out_specs=ANY,
+            scratch_shapes=[
+                pltpu.VMEM((total * wide, LANES), f32),
+                pltpu.VMEM((1, 26, step * LANES), f32),
+                pltpu.SemaphoreType.DMA((2,)),
+            ],
+            input_output_aliases={2: 0} if other else {},
+            compiler_params=PARAMS,
+            name="outer",
+        )(halo, part, out)
     return out.transpose(1, 0, 2)
 
 

time: 11.8 us -> 10.8 us (0.915)
  waiting for transfers between devices: 3.16 us -> 1.72 us
  starting transfers between devices: 5.18 us -> 5.5 us
    ppermute x6 -> x7, waiting for transfers between devices: 3.16 us -> 1.72 us  [permute(): return lax.ppermute(value, ('member', 'tile'), pairs)]
    ppermute x6 -> x7, starting transfers between devices: 5.18 us -> 5.5 us  [permute(): return lax.ppermute(value, ('member', 'tile'), pairs)]
    pallas_call x2 -> x3, Pallas kernels: 2.25 us -> 2.32 us  [the longest x2 1.78 us: local(): pl.pallas_call(functools.partial(half_kernel, wide, step, total, other),...]
  transfers between devices with their start and end apart: 6 -> 7, of which waited for: 4 -> 6; matrix products, arithmetic and copies ran while one was open for 0% -> 0% of each run, Pallas kernels for 12% -> 15%
where the time goes in v4:
time: 10.8 us; the launch traced here: 10.6 us
  starting transfers between devices  5.5 us (51%)
  Pallas kernels  2.44 us (23%)
  waiting for transfers between devices  1.72 us (16%)
  local copies, waits for them, and re-layouts  0.91 us (8%)
    ppermute x7, starting transfers between devices, permute(): return lax.ppermute(value, ('member', 'tile'), pairs)  5.5 us
    pallas_call x2, Pallas kernels, local(): pl.pallas_call(functools.partial(half_kernel, wide, step, total, other),...  1.78 us
    ppermute x7, waiting for transfers between devices, permute(): return lax.ppermute(value, ('member', 'tile'), pairs)  1.72 us
    unnamed x2, local copies, waits for them, and re-layouts  0.91 us
    pallas_call x1, Pallas kernels, local(): pl.pallas_call(functools.partial(inner_kernel, mloc, width, step, total),...  0.54 us
  transfers between devices with their start and end apart: 7, of which 6 were waited for; matrix products, arithmetic and copies ran while one was open for 0% of the time, Pallas kernels for 15%

profile of v4, /device:TPU:0, one launch (start us, length us, event | category | flops | bytes accessed | tf_op | source)
XLA Modules:
  0.0 10.6 jit_solution(17205979907527565108)
XLA Ops:
  0.0 0.5 %collective-permute-start = (f32[6,48,128]{2,1,0:T(8,128)}, f32[6,48,128]{2,1,0:T(8,128)S(1)}, u32[]{:S(2)}, u32[]{:S(2)}) collective-permute-start(f32[6,48,128]{2,1,0:T(8,128)} %bitcast.6), channel_id=1, source_target_pairs={{0,8},{1,9},{2,10},{3,11},{4,12},{5,13},{6,14},{7,15},{8,0},{9,1},... | collective-permute-start | bytes 442376 | tf_op jit(solution)/shard_map/ppermute | solution.py:27
  0.5 0.0 copy-start
  0.5 0.9 %copy-done = f32[2,6,3072]{2,0,1:T(2,128)S(1)} copy-done((f32[2,6,3072]{2,0,1:T(2,128)S(1)}, f32[2,6,3072]{2,0,1:T(2,128)}, u32[]{:S(2)}) %copy-start) | copy-done | bytes 147480
  1.4 2.7 %collective-permute-start.3 = (bf16[6,32,128]{2,1,0:T(8,128)(2,1)S(1)}, bf16[6,32,128]{2,1,0:T(8,128)(2,1)S(1)}, u32[]{:S(2)}, u32[]{:S(2)}) collective-permute-start(bf16[6,32,128]{2,1,0:T(8,128)(2,1)S(1)} %get-tuple-element.24), channel_id=1, source_target_pairs={{0,24},{1,25},{2,26},{3,27},{4,28},{5,29},{6,30},{7,31},{8,16},{9,... | collective-permute-start | bytes 147464 | tf_op jit(solution)/shard_map/ppermute | solution.py:27
  4.1 0.0 collective-permute-done.theirs
  4.1 1.2 %collective-permute-start.1 = (bf16[64,128]{1,0:T(8,128)(2,1)S(1)}, bf16[64,128]{1,0:T(8,128)(2,1)S(1)}, u32[]{:S(2)}, u32[]{:S(2)}) collective-permute-start(bf16[64,128]{1,0:T(8,128)(2,1)S(1)} %get-tuple-element.22), channel_id=1, source_target_pairs={{0,25},{1,26},{2,27},{3,28},{4,29},{5,30},{6,31},{7,23},{8,24},{9,... | collective-permute-start | bytes 49160 | tf_op jit(solution)/shard_map/ppermute | solution.py:27
  5.3 0.5 %collective-permute-start.2 = (bf16[64,128]{1,0:T(8,128)(2,1)S(1)}, bf16[64,128]{1,0:T(8,128)(2,1)S(1)}, u32[]{:S(2)}, u32[]{:S(2)}) collective-permute-start(bf16[64,128]{1,0:T(8,128)(2,1)S(1)} %get-tuple-element.23), channel_id=1, source_target_pairs={{0,9},{1,10},{2,11},{3,12},{4,13},{5,14},{6,15},{7,23},{8,24},{9,0... | collective-permute-start | bytes 49160 | tf_op jit(solution)/shard_map/ppermute | solution.py:27
  5.8 0.4 %collective-permute-done.3.refs_0_ = bf16[6,32,128]{2,1,0:T(8,128)(2,1)S(1)} collective-permute-done((bf16[6,32,128]{2,1,0:T(8,128)(2,1)S(1)}, bf16[6,32,128]{2,1,0:T(8,128)(2,1)S(1)}, u32[]{:S(2)}, u32[]{:S(2)}) %collective-permute-start.3) | collective-permute-done | bytes 49184 | tf_op jit(solution)/shard_map/ppermute | solution.py:27
  6.2 0.2 %collective-permute-start.4 = (bf16[1,60,128]{2,1,0:T(8,128)(2,1)S(1)}, bf16[1,60,128]{2,1,0:T(8,128)(2,1)S(1)}, u32[]{:S(2)}, u32[]{:S(2)}) collective-permute-start(bf16[1,60,128]{2,1,0:T(8,128)(2,1)S(1)} %get-tuple-element.30), channel_id=1, source_target_pairs={{0,8},{1,9},{2,10},{3,11},{4,12},{5,13},{6,14},{7,15},{8,0},{9,1},... | collective-permute-start | bytes 46088 | tf_op jit(solution)/shard_map/ppermute | solution.py:27
  6.4 0.4 %collective-permute-start.5 = (bf16[1,60,128]{2,1,0:T(8,128)(2,1)S(1)}, bf16[1,60,128]{2,1,0:T(8,128)(2,1)S(1)}, u32[]{:S(2)}, u32[]{:S(2)}) collective-permute-start(bf16[1,60,128]{2,1,0:T(8,128)(2,1)S(1)} %get-tuple-element.31), channel_id=1, source_target_pairs={{0,8},{1,9},{2,10},{3,11},{4,12},{5,13},{6,14},{7,15},{8,0},{9,1},... | collective-permute-start | bytes 46088 | tf_op jit(solution)/shard_map/ppermute | solution.py:27
  6.8 0.6 %collective-permute-done.4.refs_2_ = bf16[1,60,128]{2,1,0:T(8,128)(2,1)S(1)} collective-permute-done((bf16[1,60,128]{2,1,0:T(8,128)(2,1)S(1)}, bf16[1,60,128]{2,1,0:T(8,128)(2,1)S(1)}, u32[]{:S(2)}, u32[]{:S(2)}) %collective-permute-start.4) | collective-permute-done | bytes 15392 | tf_op jit(solution)/shard_map/ppermute | solution.py:27
  7.5 0.2 %collective-permute-done.5.refs_3_ = bf16[1,60,128]{2,1,0:T(8,128)(2,1)S(1)} collective-permute-done((bf16[1,60,128]{2,1,0:T(8,128)(2,1)S(1)}, bf16[1,60,128]{2,1,0:T(8,128)(2,1)S(1)}, u32[]{:S(2)}, u32[]{:S(2)}) %collective-permute-start.5) | collective-permute-done | bytes 15392 | tf_op jit(solution)/shard_map/ppermute | solution.py:27
  7.6 0.5 %inner.1 = (f32[4,26,768]{2,1,0:T(8,128)S(1)}, f32[1,4,6,8,128]{4,3,2,1,0:T(8,128)S(1)}) custom-call(bf16[6,40,128]{2,1,0:T(8,128)(2,1)S(1)} %block.1, bf16[1,60,128]{2,1,0:T(8,128)(2,1)S(1)} %get-tuple-element.28.refs_0_, bf16[1,60,128]{2,1,0:T(8,128)(2,1)S(1)} %get-tuple-element.29.refs_1_, bf16[1,60,128]{2,1,0:T(8,128)(2,1)S(1)} %collective-permute-done.4.refs_2_, ...), custom_call_target="tpu_custom_call" | custom-call | tf_op jit(solution)/shard_map/inner/pallas_call | solution.py:279
  8.2 0.1 collective-permute-done.1.refs_0_
  8.2 0.3 %collective-permute-done.2.refs_1_ = bf16[64,128]{1,0:T(8,128)(2,1)S(1)} collective-permute-done((bf16[64,128]{1,0:T(8,128)(2,1)S(1)}, bf16[64,128]{1,0:T(8,128)(2,1)S(1)}, u32[]{:S(2)}, u32[]{:S(2)}) %collective-permute-start.2) | collective-permute-done | bytes 16416 | tf_op jit(solution)/shard_map/ppermute | solution.py:27
  8.5 0.1 collective-permute-start.6
  8.6 0.9 %outer.2.source = f32[6,26,768]{2,1,0:T(8,128)} custom-call(bf16[128,128]{1,0:T(8,128)(2,1)S(1)} %join.1.halo, f32[1,4,6,8,128]{4,3,2,1,0:T(8,128)S(1)} %get-tuple-element.35.part, f32[4,26,768]{2,1,0:T(8,128)S(1)} %get-tuple-element.36.source), custom_call_target="tpu_custom_call" | custom-call | tf_op jit(solution)/shard_map/outer/pallas_call | solution.py:301
  9.5 0.2 %collective-permute-done.6.halo = bf16[128,128]{1,0:T(8,128)(2,1)S(1)} collective-permute-done((bf16[128,128]{1,0:T(8,128)(2,1)S(1)}, bf16[128,128]{1,0:T(8,128)(2,1)S(1)}, u32[]{:S(2)}, u32[]{:S(2)}) %collective-permute-start.6) | collective-permute-done | bytes 32800 | tf_op jit(solution)/shard_map/ppermute | solution.py:27
  9.7 0.9 %outer.3 = f32[6,26,768]{2,1,0:T(8,128)} custom-call(bf16[128,128]{1,0:T(8,128)(2,1)S(1)} %collective-permute-done.6.halo, f32[1,4,6,8,128]{4,3,2,1,0:T(8,128)S(1)} %get-tuple-element.35.part, f32[6,26,768]{2,1,0:T(8,128)} %outer.2.source), custom_call_target="tpu_custom_call", output_to_operand_aliasing={{}: (2, {})} | custom-call | tf_op jit(solution)/shard_map/outer/pallas_call | solution.py:301
  (5 shorter events, 0.1 us)
Async XLA Ops:
  0.0 4.1 %collective-permute-start = (f32[6,48,128]{2,1,0:T(8,128)}, f32[6,48,128]{2,1,0:T(8,128)S(1)}, u32[]{:S(2)}, u32[]{:S(2)}) collective-permute-start(f32[6,48,128]{2,1,0:T(8,128)} %bitcast.6), channel_id=1, source_target_pairs={{0,8},{1,9},{2,10},{3,11},{4,12},{5,13},{6,14},{7,15},{8,0},{9,1},... | collective-permute-start | bytes 442376 | tf_op jit(solution)/shard_map/ppermute | solution.py:27
  0.5 0.9 %copy-start = (f32[2,6,3072]{2,0,1:T(2,128)S(1)}, f32[2,6,3072]{2,0,1:T(2,128)}, u32[]{:S(2)}) copy-start(f32[2,6,3072]{2,0,1:T(2,128)} %param.1) | copy-start | bytes 442372
  1.4 4.8 %collective-permute-start.3 = (bf16[6,32,128]{2,1,0:T(8,128)(2,1)S(1)}, bf16[6,32,128]{2,1,0:T(8,128)(2,1)S(1)}, u32[]{:S(2)}, u32[]{:S(2)}) collective-permute-start(bf16[6,32,128]{2,1,0:T(8,128)(2,1)S(1)} %get-tuple-element.24), channel_id=1, source_target_pairs={{0,24},{1,25},{2,26},{3,27},{4,28},{5,29},{6,30},{7,31},{8,16},{9,... | collective-permute-start | bytes 147464 | tf_op jit(solution)/shard_map/ppermute | solution.py:27
  4.1 4.1 %collective-permute-start.1 = (bf16[64,128]{1,0:T(8,128)(2,1)S(1)}, bf16[64,128]{1,0:T(8,128)(2,1)S(1)}, u32[]{:S(2)}, u32[]{:S(2)}) collective-permute-start(bf16[64,128]{1,0:T(8,128)(2,1)S(1)} %get-tuple-element.22), channel_id=1, source_target_pairs={{0,25},{1,26},{2,27},{3,28},{4,29},{5,30},{6,31},{7,23},{8,24},{9,... | collective-permute-start | bytes 49160 | tf_op jit(solution)/shard_map/ppermute | solution.py:27
  5.3 3.2 %collective-permute-start.2 = (bf16[64,128]{1,0:T(8,128)(2,1)S(1)}, bf16[64,128]{1,0:T(8,128)(2,1)S(1)}, u32[]{:S(2)}, u32[]{:S(2)}) collective-permute-start(bf16[64,128]{1,0:T(8,128)(2,1)S(1)} %get-tuple-element.23), channel_id=1, source_target_pairs={{0,9},{1,10},{2,11},{3,12},{4,13},{5,14},{6,15},{7,23},{8,24},{9,0... | collective-permute-start | bytes 49160 | tf_op jit(solution)/shard_map/ppermute | solution.py:27
  6.2 1.2 %collective-permute-start.4 = (bf16[1,60,128]{2,1,0:T(8,128)(2,1)S(1)}, bf16[1,60,128]{2,1,0:T(8,128)(2,1)S(1)}, u32[]{:S(2)}, u32[]{:S(2)}) collective-permute-start(bf16[1,60,128]{2,1,0:T(8,128)(2,1)S(1)} %get-tuple-element.30), channel_id=1, source_target_pairs={{0,8},{1,9},{2,10},{3,11},{4,12},{5,13},{6,14},{7,15},{8,0},{9,1},... | collective-permute-start | bytes 46088 | tf_op jit(solution)/shard_map/ppermute | solution.py:27
  6.4 1.2 %collective-permute-start.5 = (bf16[1,60,128]{2,1,0:T(8,128)(2,1)S(1)}, bf16[1,60,128]{2,1,0:T(8,128)(2,1)S(1)}, u32[]{:S(2)}, u32[]{:S(2)}) collective-permute-start(bf16[1,60,128]{2,1,0:T(8,128)(2,1)S(1)} %get-tuple-element.31), channel_id=1, source_target_pairs={{0,8},{1,9},{2,10},{3,11},{4,12},{5,13},{6,14},{7,15},{8,0},{9,1},... | collective-permute-start | bytes 46088 | tf_op jit(solution)/shard_map/ppermute | solution.py:27
  8.5 1.2 %collective-permute-start.6 = (bf16[128,128]{1,0:T(8,128)(2,1)S(1)}, bf16[128,128]{1,0:T(8,128)(2,1)S(1)}, u32[]{:S(2)}, u32[]{:S(2)}) collective-permute-start(bf16[128,128]{1,0:T(8,128)(2,1)S(1)} %join.1.halo), channel_id=1, source_target_pairs={{0,8},{1,9},{2,10},{3,11},{4,12},{5,13},{6,14},{7,15},{8,0},{9,1},... | collective-permute-start | bytes 98312 | tf_op jit(solution)/shard_map/ppermute | solution.py:27

commit v5 on v4

--- a/solution.py
+++ b/solution.py
@@ -46,8 +46,13 @@
     out[:, LEAD + rows : LEAD + rows + LEAD, :] = fill
 
 
-def start_kernel(mloc, wide, step, src, ours, *sends):
+def mark_kernel(out):
+    out[...] = jnp.full(out.shape, PAD, out.dtype)
+
+
+def start_kernel(mloc, wide, step, src, early, ours, *sends):
     load_kernel(src, ours)
+    ours[0, 0:LEAD, :] = early[...]
     pair = lax.axis_index("member") // 2
     for q, send in enumerate(sends):
         base = (pair ^ (q + 1)) * (2 * step * mloc) + LEAD - EDGE * mloc
@@ -232,15 +237,23 @@
     view = fields.reshape(mloc, planes, spread, LANES).transpose(1, 2, 0, 3)
     view = view.reshape(planes, spread * mloc, LANES)
     padded = (planes, spread * mloc + 2 * LEAD, LANES)
+    early = pl.pallas_call(
+        mark_kernel,
+        out_shape=jax.ShapeDtypeStruct((8, LANES), f32),
+        out_specs=VMEM,
+        compiler_params=PARAMS,
+        cost_estimate=pl.CostEstimate(flops=1 << 36, bytes_accessed=1 << 24, transcendentals=0),
+        name="mark",
+    )()
     ours, *sends = pl.pallas_call(
         functools.partial(start_kernel, mloc, wide, step),
         out_shape=[jax.ShapeDtypeStruct(padded, f32)]
         + [jax.ShapeDtypeStruct((planes, mloc * wide, LANES), bf16)] * (half - 1),
-        in_specs=[VMEM],
+        in_specs=[VMEM, VMEM],
         out_specs=[VMEM] * half,
         compiler_params=PARAMS,
         name="load",
-    )(view)
+    )(view, early)
     both, *edges = pl.pallas_call(
         functools.partial(edges_kernel, mloc, wide, step),
         out_shape=[jax.ShapeDtypeStruct((2,) + padded, f32)]

time: 10.8 us -> 10.8 us (level)
  local copies, waits for them, and re-layouts: 0.91 us -> 0.45 us
  starting transfers between devices: 5.5 us -> 5.85 us
    unnamed x2, local copies, waits for them, and re-layouts: 0.91 us -> 0.45 us
    ppermute x7, starting transfers between devices: 5.5 us -> 5.85 us  [permute(): return lax.ppermute(value, ('member', 'tile'), pairs)]
  transfers between devices with their start and end apart: 7 -> 7, of which waited for: 6 -> 4; matrix products, arithmetic and copies ran while one was open for 0% -> 0% of each run, Pallas kernels for 15% -> 15%
where the time goes in v5:
time: 10.8 us; the launch traced here: 10.6 us
  starting transfers between devices  5.85 us (54%)
  Pallas kernels  2.45 us (23%)
  waiting for transfers between devices  1.8 us (17%)
  local copies, waits for them, and re-layouts  0.45 us (4%)
    ppermute x7, starting transfers between devices, permute(): return lax.ppermute(value, ('member', 'tile'), pairs)  5.85 us
    ppermute x7, waiting for transfers between devices, permute(): return lax.ppermute(value, ('member', 'tile'), pairs)  1.8 us
    pallas_call x2, Pallas kernels, local(): pl.pallas_call(functools.partial(half_kernel, wide, step, total, other),...  1.79 us
    pallas_call x1, Pallas kernels, local(): pl.pallas_call(functools.partial(inner_kernel, mloc, width, step, total),...  0.54 us
    unnamed x2, local copies, waits for them, and re-layouts  0.45 us
  transfers between devices with their start and end apart: 7, of which 4 were waited for; matrix products, arithmetic and copies ran while one was open for 0% of the time, Pallas kernels for 15%

profile of v5, /device:TPU:0, one launch (start us, length us, event | category | flops | bytes accessed | tf_op | source)
XLA Modules:
  0.0 10.6 jit_solution(9154883830107252112)
XLA Ops:
  0.0 0.0 copy-start
  0.0 0.5 %collective-permute-start = (f32[6,48,128]{2,1,0:T(8,128)}, f32[6,48,128]{2,1,0:T(8,128)S(1)}, u32[]{:S(2)}, u32[]{:S(2)}) collective-permute-start(f32[6,48,128]{2,1,0:T(8,128)} %bitcast.6), channel_id=1, source_target_pairs={{0,8},{1,9},{2,10},{3,11},{4,12},{5,13},{6,14},{7,15},{8,0},{9,1},... | collective-permute-start | bytes 442376 | tf_op jit(solution)/shard_map/ppermute | solution.py:27
  0.5 0.5 %copy-done = f32[2,6,3072]{2,0,1:T(2,128)S(1)} copy-done((f32[2,6,3072]{2,0,1:T(2,128)S(1)}, f32[2,6,3072]{2,0,1:T(2,128)}, u32[]{:S(2)}) %copy-start) | copy-done | bytes 147480
  0.9 2.4 %collective-permute-start.3 = (bf16[6,32,128]{2,1,0:T(8,128)(2,1)S(1)}, bf16[6,32,128]{2,1,0:T(8,128)(2,1)S(1)}, u32[]{:S(2)}, u32[]{:S(2)}) collective-permute-start(bf16[6,32,128]{2,1,0:T(8,128)(2,1)S(1)} %get-tuple-element.24), channel_id=1, source_target_pairs={{0,24},{1,25},{2,26},{3,27},{4,28},{5,29},{6,30},{7,31},{8,16},{9,... | collective-permute-start | bytes 147464 | tf_op jit(solution)/shard_map/ppermute | solution.py:27
  3.4 0.0 collective-permute-done.theirs
  3.4 1.9 %collective-permute-start.1 = (bf16[64,128]{1,0:T(8,128)(2,1)S(1)}, bf16[64,128]{1,0:T(8,128)(2,1)S(1)}, u32[]{:S(2)}, u32[]{:S(2)}) collective-permute-start(bf16[64,128]{1,0:T(8,128)(2,1)S(1)} %get-tuple-element.22), channel_id=1, source_target_pairs={{0,25},{1,26},{2,27},{3,28},{4,29},{5,30},{6,31},{7,23},{8,24},{9,... | collective-permute-start | bytes 49160 | tf_op jit(solution)/shard_map/ppermute | solution.py:27
  5.3 0.5 %collective-permute-start.2 = (bf16[64,128]{1,0:T(8,128)(2,1)S(1)}, bf16[64,128]{1,0:T(8,128)(2,1)S(1)}, u32[]{:S(2)}, u32[]{:S(2)}) collective-permute-start(bf16[64,128]{1,0:T(8,128)(2,1)S(1)} %get-tuple-element.23), channel_id=1, source_target_pairs={{0,9},{1,10},{2,11},{3,12},{4,13},{5,14},{6,15},{7,23},{8,24},{9,0... | collective-permute-start | bytes 49160 | tf_op jit(solution)/shard_map/ppermute | solution.py:27
  5.8 0.0 collective-permute-done.3.refs_0_
  5.9 0.1 collective-permute-start.4
  5.9 0.5 %collective-permute-start.5 = (bf16[1,60,128]{2,1,0:T(8,128)(2,1)S(1)}, bf16[1,60,128]{2,1,0:T(8,128)(2,1)S(1)}, u32[]{:S(2)}, u32[]{:S(2)}) collective-permute-start(bf16[1,60,128]{2,1,0:T(8,128)(2,1)S(1)} %get-tuple-element.31), channel_id=1, source_target_pairs={{0,8},{1,9},{2,10},{3,11},{4,12},{5,13},{6,14},{7,15},{8,0},{9,1},... | collective-permute-start | bytes 46088 | tf_op jit(solution)/shard_map/ppermute | solution.py:27
  6.5 0.6 %collective-permute-done.4.refs_2_ = bf16[1,60,128]{2,1,0:T(8,128)(2,1)S(1)} collective-permute-done((bf16[1,60,128]{2,1,0:T(8,128)(2,1)S(1)}, bf16[1,60,128]{2,1,0:T(8,128)(2,1)S(1)}, u32[]{:S(2)}, u32[]{:S(2)}) %collective-permute-start.4) | collective-permute-done | bytes 15392 | tf_op jit(solution)/shard_map/ppermute | solution.py:27
  7.1 0.2 %collective-permute-done.5.refs_3_ = bf16[1,60,128]{2,1,0:T(8,128)(2,1)S(1)} collective-permute-done((bf16[1,60,128]{2,1,0:T(8,128)(2,1)S(1)}, bf16[1,60,128]{2,1,0:T(8,128)(2,1)S(1)}, u32[]{:S(2)}, u32[]{:S(2)}) %collective-permute-start.5) | collective-permute-done | bytes 15392 | tf_op jit(solution)/shard_map/ppermute | solution.py:27
  7.3 0.5 %inner.1 = (f32[4,26,768]{2,1,0:T(8,128)S(1)}, f32[1,4,6,8,128]{4,3,2,1,0:T(8,128)S(1)}) custom-call(bf16[6,40,128]{2,1,0:T(8,128)(2,1)S(1)} %block.1, bf16[1,60,128]{2,1,0:T(8,128)(2,1)S(1)} %get-tuple-element.28.refs_0_, bf16[1,60,128]{2,1,0:T(8,128)(2,1)S(1)} %get-tuple-element.29.refs_1_, bf16[1,60,128]{2,1,0:T(8,128)(2,1)S(1)} %collective-permute-done.4.refs_2_, ...), custom_call_target="tpu_custom_call" | custom-call | tf_op jit(solution)/shard_map/inner/pallas_call | solution.py:292
  7.8 0.0 collective-permute-done.1.refs_0_
  7.8 0.7 %collective-permute-done.2.refs_1_ = bf16[64,128]{1,0:T(8,128)(2,1)S(1)} collective-permute-done((bf16[64,128]{1,0:T(8,128)(2,1)S(1)}, bf16[64,128]{1,0:T(8,128)(2,1)S(1)}, u32[]{:S(2)}, u32[]{:S(2)}) %collective-permute-start.2) | collective-permute-done | bytes 16416 | tf_op jit(solution)/shard_map/ppermute | solution.py:27
  8.5 0.0 collective-permute-start.6
  8.5 0.9 %outer.2.source = f32[6,26,768]{2,1,0:T(8,128)} custom-call(bf16[128,128]{1,0:T(8,128)(2,1)S(1)} %join.1.halo, f32[1,4,6,8,128]{4,3,2,1,0:T(8,128)S(1)} %get-tuple-element.35.part, f32[4,26,768]{2,1,0:T(8,128)S(1)} %get-tuple-element.36.source), custom_call_target="tpu_custom_call" | custom-call | tf_op jit(solution)/shard_map/outer/pallas_call | solution.py:314
  9.4 0.3 %collective-permute-done.6.halo = bf16[128,128]{1,0:T(8,128)(2,1)S(1)} collective-permute-done((bf16[128,128]{1,0:T(8,128)(2,1)S(1)}, bf16[128,128]{1,0:T(8,128)(2,1)S(1)}, u32[]{:S(2)}, u32[]{:S(2)}) %collective-permute-start.6) | collective-permute-done | bytes 32800 | tf_op jit(solution)/shard_map/ppermute | solution.py:27
  9.7 0.9 %outer.3 = f32[6,26,768]{2,1,0:T(8,128)} custom-call(bf16[128,128]{1,0:T(8,128)(2,1)S(1)} %collective-permute-done.6.halo, f32[1,4,6,8,128]{4,3,2,1,0:T(8,128)S(1)} %get-tuple-element.35.part, f32[6,26,768]{2,1,0:T(8,128)} %outer.2.source), custom_call_target="tpu_custom_call", output_to_operand_aliasing={{}: (2, {})} | custom-call | tf_op jit(solution)/shard_map/outer/pallas_call | solution.py:314
  (6 shorter events, 0.1 us)
Async XLA Ops:
  0.0 0.9 %copy-start = (f32[2,6,3072]{2,0,1:T(2,128)S(1)}, f32[2,6,3072]{2,0,1:T(2,128)}, u32[]{:S(2)}) copy-start(f32[2,6,3072]{2,0,1:T(2,128)} %param.1) | copy-start | bytes 442372
  0.0 3.4 %collective-permute-start = (f32[6,48,128]{2,1,0:T(8,128)}, f32[6,48,128]{2,1,0:T(8,128)S(1)}, u32[]{:S(2)}, u32[]{:S(2)}) collective-permute-start(f32[6,48,128]{2,1,0:T(8,128)} %bitcast.6), channel_id=1, source_target_pairs={{0,8},{1,9},{2,10},{3,11},{4,12},{5,13},{6,14},{7,15},{8,0},{9,1},... | collective-permute-start | bytes 442376 | tf_op jit(solution)/shard_map/ppermute | solution.py:27
  0.9 4.9 %collective-permute-start.3 = (bf16[6,32,128]{2,1,0:T(8,128)(2,1)S(1)}, bf16[6,32,128]{2,1,0:T(8,128)(2,1)S(1)}, u32[]{:S(2)}, u32[]{:S(2)}) collective-permute-start(bf16[6,32,128]{2,1,0:T(8,128)(2,1)S(1)} %get-tuple-element.24), channel_id=1, source_target_pairs={{0,24},{1,25},{2,26},{3,27},{4,28},{5,29},{6,30},{7,31},{8,16},{9,... | collective-permute-start | bytes 147464 | tf_op jit(solution)/shard_map/ppermute | solution.py:27
  3.4 4.4 %collective-permute-start.1 = (bf16[64,128]{1,0:T(8,128)(2,1)S(1)}, bf16[64,128]{1,0:T(8,128)(2,1)S(1)}, u32[]{:S(2)}, u32[]{:S(2)}) collective-permute-start(bf16[64,128]{1,0:T(8,128)(2,1)S(1)} %get-tuple-element.22), channel_id=1, source_target_pairs={{0,25},{1,26},{2,27},{3,28},{4,29},{5,30},{6,31},{7,23},{8,24},{9,... | collective-permute-start | bytes 49160 | tf_op jit(solution)/shard_map/ppermute | solution.py:27
  5.3 3.2 %collective-permute-start.2 = (bf16[64,128]{1,0:T(8,128)(2,1)S(1)}, bf16[64,128]{1,0:T(8,128)(2,1)S(1)}, u32[]{:S(2)}, u32[]{:S(2)}) collective-permute-start(bf16[64,128]{1,0:T(8,128)(2,1)S(1)} %get-tuple-element.23), channel_id=1, source_target_pairs={{0,9},{1,10},{2,11},{3,12},{4,13},{5,14},{6,15},{7,23},{8,24},{9,0... | collective-permute-start | bytes 49160 | tf_op jit(solution)/shard_map/ppermute | solution.py:27
  5.9 1.2 %collective-permute-start.4 = (bf16[1,60,128]{2,1,0:T(8,128)(2,1)S(1)}, bf16[1,60,128]{2,1,0:T(8,128)(2,1)S(1)}, u32[]{:S(2)}, u32[]{:S(2)}) collective-permute-start(bf16[1,60,128]{2,1,0:T(8,128)(2,1)S(1)} %get-tuple-element.30), channel_id=1, source_target_pairs={{0,8},{1,9},{2,10},{3,11},{4,12},{5,13},{6,14},{7,15},{8,0},{9,1},... | collective-permute-start | bytes 46088 | tf_op jit(solution)/shard_map/ppermute | solution.py:27
  5.9 1.3 %collective-permute-start.5 = (bf16[1,60,128]{2,1,0:T(8,128)(2,1)S(1)}, bf16[1,60,128]{2,1,0:T(8,128)(2,1)S(1)}, u32[]{:S(2)}, u32[]{:S(2)}) collective-permute-start(bf16[1,60,128]{2,1,0:T(8,128)(2,1)S(1)} %get-tuple-element.31), channel_id=1, source_target_pairs={{0,8},{1,9},{2,10},{3,11},{4,12},{5,13},{6,14},{7,15},{8,0},{9,1},... | collective-permute-start | bytes 46088 | tf_op jit(solution)/shard_map/ppermute | solution.py:27
  8.5 1.2 %collective-permute-start.6 = (bf16[128,128]{1,0:T(8,128)(2,1)S(1)}, bf16[128,128]{1,0:T(8,128)(2,1)S(1)}, u32[]{:S(2)}, u32[]{:S(2)}) collective-permute-start(bf16[128,128]{1,0:T(8,128)(2,1)S(1)} %join.1.halo), channel_id=1, source_target_pairs={{0,8},{1,9},{2,10},{3,11},{4,12},{5,13},{6,14},{7,15},{8,0},{9,1},... | collective-permute-start | bytes 98312 | tf_op jit(solution)/shard_map/ppermute | solution.py:27

commit v6 on v5

--- a/solution.py
+++ b/solution.py
@@ -28,14 +28,21 @@
 
 
 def beside(q, members, tiles, m, t):
-    up = m % 2 == 0
-    if t == (tiles - 1 if up else 0):
+    ends, near, swap = (0, tiles - 1), t ^ 1, m ^ (2 * q)
+    if t in ends:
+        if (m % 2 == 0) == (q == 0):
+            return swap & ~1, near
         return m ^ (2 * q if q else members // 2), t
-    return m ^ (2 * q + 1), (t + 1 if up else t - 1)
-
-
-def edge_side():
-    return lax.axis_index("member") % 2
+    if m % 2 == 0:
+        return (swap | 1 if q and near in ends else swap), near
+    return swap, (t + 1 if t % 2 else t - 1)
+
+
+def place():
+    core, tile, tiles = lax.axis_index("member") % 2, lax.axis_index("tile"), lax.axis_size("tile")
+    last = jnp.logical_or(tile == 0, tile == tiles - 1)
+    inside = (core + tile + 1) % 2
+    return core, last, jnp.where(last, (tile == 0).astype(jnp.int32), inside)
 
 
 def load_kernel(src, out):
@@ -76,7 +83,7 @@
 def edges_kernel(mloc, wide, step, theirs, ours, both, *edges):
     spread_kernel(theirs, ours, both)
     pair = lax.axis_index("member") // 2
-    plane = (ours.shape[0] - 1) * (1 - edge_side())
+    plane = (ours.shape[0] - 1) * place()[2]
     for q, edge in enumerate(edges):
         edge[...] = window(both, mloc, plane, (pair ^ q) * (2 * step), wide)
 
@@ -194,21 +201,31 @@
             part[group, 3, j] = layers[-1][1][j]
 
 
-def half_kernel(wide, step, total, other, halo, part, source, out, stage, tile_out, sem):
+def half_kernel(wide, step, total, own, *refs):
+    *halos, part, source, out, stage, tile_out, sem = refs
     planes = out.shape[0]
-    tile, tiles = lax.axis_index("tile"), lax.axis_size("tile")
-    end = edge_side() if other else 1 - edge_side()
-    start = (lax.axis_index("member") % 2) * step
+    core, last, toward = place()
+    later = len(halos) == 2
+    end = jnp.where(last, toward, 1 - toward) if later else jnp.where(last, 1 - toward, toward)
+    start = core * step
     bias = end.astype(jnp.float32) * 18.0
     copies = []
-    if not other:
+    if later:
+        got, other = halos
+        stage[...] = other[...].astype(jnp.float32)
+        for rows, owner in ((slice(0, own), 0), (slice(own, got.shape[0]), 1)):
+
+            @pl.when(jnp.logical_and(last, core == owner))
+            def _():
+                stage[rows, :] = got[rows, :].astype(jnp.float32)
+    else:
         copies.append(pltpu.make_async_copy(source, out.at[pl.ds(1, planes - 2)], sem.at[0]))
         copies[0].start()
-    stage[...] = halo[...].astype(jnp.float32)
-
-    @pl.when(tile == end * (tiles - 1))
-    def _():
-        stage[...] = jnp.full(stage.shape, PAD, jnp.float32)
+        stage[...] = halos[0][...].astype(jnp.float32)
+
+        @pl.when(last)
+        def _():
+            stage[...] = jnp.full(stage.shape, PAD, jnp.float32)
 
     for group in range(total // 8):
         keys, _ = keys_of(stage, None, group, wide, step, start)
@@ -310,21 +327,22 @@
     )(*got[::-1])
     other = swap(got)
     out = inner
-    for other, halo in enumerate((got, other)):
+    for halos in ((got,), (got, other)):
+        later = len(halos) == 2
         out = pl.pallas_call(
-            functools.partial(half_kernel, wide, step, total, other),
+            functools.partial(half_kernel, wide, step, total, 2 * mloc * wide),
             out_shape=out_shape,
-            in_specs=[VMEM, VMEM, ANY if other else VMEM],
+            in_specs=[VMEM] * (len(halos) + 1) + [ANY if later else VMEM],
             out_specs=ANY,
             scratch_shapes=[
                 pltpu.VMEM((total * wide, LANES), f32),
                 pltpu.VMEM((1, 26, step * LANES), f32),
                 pltpu.SemaphoreType.DMA((2,)),
             ],
-            input_output_aliases={2: 0} if other else {},
+            input_output_aliases={3: 0} if later else {},
             compiler_params=PARAMS,
             name="outer",
-        )(halo, part, out)
+        )(*halos, part, out)
     return out.transpose(1, 0, 2)
 
 

time: 10.8 us -> 10.8 us (level)
  starting transfers between devices: 5.85 us -> 5.96 us
    ppermute x7, starting transfers between devices: 5.85 us -> 5.96 us  [permute(): return lax.ppermute(value, ('member', 'tile'), pairs)]
  transfers between devices with their start and end apart: 7 -> 7, of which waited for: 4 -> 4; matrix products, arithmetic and copies ran while one was open for 0% -> 0% of each run, Pallas kernels for 15% -> 14%
where the time goes in v6:
time: 10.8 us; the launch traced here: 10.7 us
  starting transfers between devices  5.96 us (55%)
  Pallas kernels  2.45 us (23%)
  waiting for transfers between devices  1.74 us (16%)
  local copies, waits for them, and re-layouts  0.45 us (4%)
    ppermute x7, starting transfers between devices, permute(): return lax.ppermute(value, ('member', 'tile'), pairs)  5.96 us
    pallas_call x2, Pallas kernels, local(): pl.pallas_call(functools.partial(half_kernel, wide, step, total, 2 * mloc...  1.79 us
    ppermute x7, waiting for transfers between devices, permute(): return lax.ppermute(value, ('member', 'tile'), pairs)  1.74 us
    pallas_call x1, Pallas kernels, local(): pl.pallas_call(functools.partial(inner_kernel, mloc, width, step, total),...  0.54 us
    unnamed x2, local copies, waits for them, and re-layouts  0.45 us
  transfers between devices with their start and end apart: 7, of which 4 were waited for; matrix products, arithmetic and copies ran while one was open for 0% of the time, Pallas kernels for 14%

profile of v6, /device:TPU:0, one launch (start us, length us, event | category | flops | bytes accessed | tf_op | source)
XLA Modules:
  0.0 10.7 jit_solution(3001943486864048563)
XLA Ops:
  0.0 0.0 copy-start
  0.0 0.5 %collective-permute-start = (f32[6,48,128]{2,1,0:T(8,128)}, f32[6,48,128]{2,1,0:T(8,128)S(1)}, u32[]{:S(2)}, u32[]{:S(2)}) collective-permute-start(f32[6,48,128]{2,1,0:T(8,128)} %bitcast.6), channel_id=1, source_target_pairs={{0,8},{1,9},{2,10},{3,11},{4,12},{5,13},{6,14},{7,15},{8,0},{9,1},... | collective-permute-start | bytes 442376 | tf_op jit(solution)/shard_map/ppermute | solution.py:27
  0.5 0.5 %copy-done = f32[2,6,3072]{2,0,1:T(2,128)S(1)} copy-done((f32[2,6,3072]{2,0,1:T(2,128)S(1)}, f32[2,6,3072]{2,0,1:T(2,128)}, u32[]{:S(2)}) %copy-start) | copy-done | bytes 147480
  0.9 2.4 %collective-permute-start.3 = (bf16[6,32,128]{2,1,0:T(8,128)(2,1)S(1)}, bf16[6,32,128]{2,1,0:T(8,128)(2,1)S(1)}, u32[]{:S(2)}, u32[]{:S(2)}) collective-permute-start(bf16[6,32,128]{2,1,0:T(8,128)(2,1)S(1)} %get-tuple-element.24), channel_id=1, source_target_pairs={{0,24},{1,25},{2,26},{3,27},{4,28},{5,29},{6,30},{7,31},{8,16},{9,... | collective-permute-start | bytes 147464 | tf_op jit(solution)/shard_map/ppermute | solution.py:27
  3.4 0.0 collective-permute-done.theirs
  3.4 1.2 %collective-permute-start.1 = (bf16[64,128]{1,0:T(8,128)(2,1)S(1)}, bf16[64,128]{1,0:T(8,128)(2,1)S(1)}, u32[]{:S(2)}, u32[]{:S(2)}) collective-permute-start(bf16[64,128]{1,0:T(8,128)(2,1)S(1)} %get-tuple-element.22), channel_id=1, source_target_pairs={{0,16},{1,24},{2,19},{3,18},{4,21},{5,20},{6,31},{7,23},{8,17},{9,... | collective-permute-start | bytes 49160 | tf_op jit(solution)/shard_map/ppermute | solution.py:27
  4.6 1.2 %collective-permute-start.2 = (bf16[64,128]{1,0:T(8,128)(2,1)S(1)}, bf16[64,128]{1,0:T(8,128)(2,1)S(1)}, u32[]{:S(2)}, u32[]{:S(2)}) collective-permute-start(bf16[64,128]{1,0:T(8,128)(2,1)S(1)} %get-tuple-element.23), channel_id=1, source_target_pairs={{0,1},{1,0},{2,3},{3,2},{4,5},{5,4},{6,7},{7,6},{8,24},{9,10},{10,... | collective-permute-start | bytes 49160 | tf_op jit(solution)/shard_map/ppermute | solution.py:27
  5.9 0.0 collective-permute-done.3.refs_0_
  5.9 0.5 %collective-permute-start.4 = (bf16[1,60,128]{2,1,0:T(8,128)(2,1)S(1)}, bf16[1,60,128]{2,1,0:T(8,128)(2,1)S(1)}, u32[]{:S(2)}, u32[]{:S(2)}) collective-permute-start(bf16[1,60,128]{2,1,0:T(8,128)(2,1)S(1)} %get-tuple-element.30), channel_id=1, source_target_pairs={{0,8},{1,9},{2,10},{3,11},{4,12},{5,13},{6,14},{7,15},{8,0},{9,1},... | collective-permute-start | bytes 46088 | tf_op jit(solution)/shard_map/ppermute | solution.py:27
  6.4 0.1 collective-permute-start.5
  6.5 0.7 %collective-permute-done.4.refs_2_ = bf16[1,60,128]{2,1,0:T(8,128)(2,1)S(1)} collective-permute-done((bf16[1,60,128]{2,1,0:T(8,128)(2,1)S(1)}, bf16[1,60,128]{2,1,0:T(8,128)(2,1)S(1)}, u32[]{:S(2)}, u32[]{:S(2)}) %collective-permute-start.4) | collective-permute-done | bytes 15392 | tf_op jit(solution)/shard_map/ppermute | solution.py:27
  7.3 0.3 %collective-permute-done.5.refs_3_ = bf16[1,60,128]{2,1,0:T(8,128)(2,1)S(1)} collective-permute-done((bf16[1,60,128]{2,1,0:T(8,128)(2,1)S(1)}, bf16[1,60,128]{2,1,0:T(8,128)(2,1)S(1)}, u32[]{:S(2)}, u32[]{:S(2)}) %collective-permute-start.5) | collective-permute-done | bytes 15392 | tf_op jit(solution)/shard_map/ppermute | solution.py:27
  7.6 0.5 %inner.1 = (f32[4,26,768]{2,1,0:T(8,128)S(1)}, f32[1,4,6,8,128]{4,3,2,1,0:T(8,128)S(1)}) custom-call(bf16[6,40,128]{2,1,0:T(8,128)(2,1)S(1)} %block.1, bf16[1,60,128]{2,1,0:T(8,128)(2,1)S(1)} %get-tuple-element.28.refs_0_, bf16[1,60,128]{2,1,0:T(8,128)(2,1)S(1)} %get-tuple-element.29.refs_1_, bf16[1,60,128]{2,1,0:T(8,128)(2,1)S(1)} %collective-permute-done.4.refs_2_, ...), custom_call_target="tpu_custom_call" | custom-call | tf_op jit(solution)/shard_map/inner/pallas_call | solution.py:309
  8.2 0.0 collective-permute-done.1.refs_0_
  8.2 0.4 %collective-permute-done.2.refs_1_ = bf16[64,128]{1,0:T(8,128)(2,1)S(1)} collective-permute-done((bf16[64,128]{1,0:T(8,128)(2,1)S(1)}, bf16[64,128]{1,0:T(8,128)(2,1)S(1)}, u32[]{:S(2)}, u32[]{:S(2)}) %collective-permute-start.2) | collective-permute-done | bytes 16416 | tf_op jit(solution)/shard_map/ppermute | solution.py:27
  8.6 0.0 collective-permute-start.6
  8.6 0.9 %outer.2.refs_3_ = f32[6,26,768]{2,1,0:T(8,128)} custom-call(bf16[128,128]{1,0:T(8,128)(2,1)S(1)} %join.1.refs_0_, f32[1,4,6,8,128]{4,3,2,1,0:T(8,128)S(1)} %get-tuple-element.35.refs_1_.refs_2_, f32[4,26,768]{2,1,0:T(8,128)S(1)} %get-tuple-element.36.refs_2_), custom_call_target="tpu_custom_call" | custom-call | tf_op jit(solution)/shard_map/outer/pallas_call | solution.py:332
  9.5 0.3 %collective-permute-done.6.refs_1_ = bf16[128,128]{1,0:T(8,128)(2,1)S(1)} collective-permute-done((bf16[128,128]{1,0:T(8,128)(2,1)S(1)}, bf16[128,128]{1,0:T(8,128)(2,1)S(1)}, u32[]{:S(2)}, u32[]{:S(2)}) %collective-permute-start.6) | collective-permute-done | bytes 32800 | tf_op jit(solution)/shard_map/ppermute | solution.py:27
  9.8 0.9 %outer.3 = f32[6,26,768]{2,1,0:T(8,128)} custom-call(bf16[128,128]{1,0:T(8,128)(2,1)S(1)} %join.1.refs_0_, bf16[128,128]{1,0:T(8,128)(2,1)S(1)} %collective-permute-done.6.refs_1_, f32[1,4,6,8,128]{4,3,2,1,0:T(8,128)S(1)} %get-tuple-element.35.refs_1_.refs_2_, f32[6,26,768]{2,1,0:T(8,128)} %outer.2.refs_3_), custom_call_target="tpu_custom_call", output_to_operand_aliasing={{}: (3, {})} | custom-call | tf_op jit(solution)/shard_map/outer/pallas_call | solution.py:332
  (6 shorter events, 0.1 us)
Async XLA Ops:
  0.0 0.9 %copy-start = (f32[2,6,3072]{2,0,1:T(2,128)S(1)}, f32[2,6,3072]{2,0,1:T(2,128)}, u32[]{:S(2)}) copy-start(f32[2,6,3072]{2,0,1:T(2,128)} %param.1) | copy-start | bytes 442372
  0.0 3.4 %collective-permute-start = (f32[6,48,128]{2,1,0:T(8,128)}, f32[6,48,128]{2,1,0:T(8,128)S(1)}, u32[]{:S(2)}, u32[]{:S(2)}) collective-permute-start(f32[6,48,128]{2,1,0:T(8,128)} %bitcast.6), channel_id=1, source_target_pairs={{0,8},{1,9},{2,10},{3,11},{4,12},{5,13},{6,14},{7,15},{8,0},{9,1},... | collective-permute-start | bytes 442376 | tf_op jit(solution)/shard_map/ppermute | solution.py:27
  0.9 4.9 %collective-permute-start.3 = (bf16[6,32,128]{2,1,0:T(8,128)(2,1)S(1)}, bf16[6,32,128]{2,1,0:T(8,128)(2,1)S(1)}, u32[]{:S(2)}, u32[]{:S(2)}) collective-permute-start(bf16[6,32,128]{2,1,0:T(8,128)(2,1)S(1)} %get-tuple-element.24), channel_id=1, source_target_pairs={{0,24},{1,25},{2,26},{3,27},{4,28},{5,29},{6,30},{7,31},{8,16},{9,... | collective-permute-start | bytes 147464 | tf_op jit(solution)/shard_map/ppermute | solution.py:27
  3.4 4.7 %collective-permute-start.1 = (bf16[64,128]{1,0:T(8,128)(2,1)S(1)}, bf16[64,128]{1,0:T(8,128)(2,1)S(1)}, u32[]{:S(2)}, u32[]{:S(2)}) collective-permute-start(bf16[64,128]{1,0:T(8,128)(2,1)S(1)} %get-tuple-element.22), channel_id=1, source_target_pairs={{0,16},{1,24},{2,19},{3,18},{4,21},{5,20},{6,31},{7,23},{8,17},{9,... | collective-permute-start | bytes 49160 | tf_op jit(solution)/shard_map/ppermute | solution.py:27
  4.6 3.9 %collective-permute-start.2 = (bf16[64,128]{1,0:T(8,128)(2,1)S(1)}, bf16[64,128]{1,0:T(8,128)(2,1)S(1)}, u32[]{:S(2)}, u32[]{:S(2)}) collective-permute-start(bf16[64,128]{1,0:T(8,128)(2,1)S(1)} %get-tuple-element.23), channel_id=1, source_target_pairs={{0,1},{1,0},{2,3},{3,2},{4,5},{5,4},{6,7},{7,6},{8,24},{9,10},{10,... | collective-permute-start | bytes 49160 | tf_op jit(solution)/shard_map/ppermute | solution.py:27
  5.9 1.4 %collective-permute-start.4 = (bf16[1,60,128]{2,1,0:T(8,128)(2,1)S(1)}, bf16[1,60,128]{2,1,0:T(8,128)(2,1)S(1)}, u32[]{:S(2)}, u32[]{:S(2)}) collective-permute-start(bf16[1,60,128]{2,1,0:T(8,128)(2,1)S(1)} %get-tuple-element.30), channel_id=1, source_target_pairs={{0,8},{1,9},{2,10},{3,11},{4,12},{5,13},{6,14},{7,15},{8,0},{9,1},... | collective-permute-start | bytes 46088 | tf_op jit(solution)/shard_map/ppermute | solution.py:27
  6.4 1.2 %collective-permute-start.5 = (bf16[1,60,128]{2,1,0:T(8,128)(2,1)S(1)}, bf16[1,60,128]{2,1,0:T(8,128)(2,1)S(1)}, u32[]{:S(2)}, u32[]{:S(2)}) collective-permute-start(bf16[1,60,128]{2,1,0:T(8,128)(2,1)S(1)} %get-tuple-element.31), channel_id=1, source_target_pairs={{0,8},{1,9},{2,10},{3,11},{4,12},{5,13},{6,14},{7,15},{8,0},{9,1},... | collective-permute-start | bytes 46088 | tf_op jit(solution)/shard_map/ppermute | solution.py:27
  8.6 1.2 %collective-permute-start.6 = (bf16[128,128]{1,0:T(8,128)(2,1)S(1)}, bf16[128,128]{1,0:T(8,128)(2,1)S(1)}, u32[]{:S(2)}, u32[]{:S(2)}) collective-permute-start(bf16[128,128]{1,0:T(8,128)(2,1)S(1)} %join.1.refs_0_), channel_id=1, source_target_pairs={{0,8},{1,9},{2,10},{3,11},{4,12},{5,13},{6,14},{7,15},{8,0},{9,1},... | collective-permute-start | bytes 98312 | tf_op jit(solution)/shard_map/ppermute | solution.py:27

commit v7 on v6

--- a/solution.py
+++ b/solution.py
@@ -80,15 +80,25 @@
     return jnp.concatenate(parts, axis=0).astype(jnp.bfloat16)
 
 
-def edges_kernel(mloc, wide, step, theirs, ours, both, *edges):
-    spread_kernel(theirs, ours, both)
+def edges_kernel(mloc, wide, step, theirs, ours, rim, *refs):
+    edges, both = refs[:-1], refs[-1]
+    core = lax.axis_index("member") % 2
     pair = lax.axis_index("member") // 2
     plane = (ours.shape[0] - 1) * place()[2]
+    rows = theirs.shape[1]
+    fill = jnp.full((LEAD, LANES), PAD, jnp.float32)
+    rim[...] = fill
+    both[core, 0] = ours[plane]
+    both[1 - core, 0, 0:LEAD, :] = fill
+    both[1 - core, 0, LEAD : LEAD + rows, :] = theirs[plane]
+    both[1 - core, 0, LEAD + rows : LEAD + rows + LEAD, :] = fill
     for q, edge in enumerate(edges):
-        edge[...] = window(both, mloc, plane, (pair ^ q) * (2 * step), wide)
-
-
-def block_kernel(mloc, width, step, both, block):
+        edge[...] = window(both, mloc, 0, (pair ^ q) * (2 * step), wide)
+
+
+def block_kernel(mloc, width, step, theirs, ours, rim, block, both):
+    spread_kernel(theirs, ours, both)
+    both[0, 0, 0:LEAD, :] = rim[...]
     start = lax.axis_index("member") * step
     for p in range(block.shape[0]):
         block[p] = window(both, mloc, p, start, width)
@@ -271,25 +281,28 @@
         compiler_params=PARAMS,
         name="load",
     )(view, early)
-    both, *edges = pl.pallas_call(
+    theirs = swap(view)
+    rim, *edges = pl.pallas_call(
         functools.partial(edges_kernel, mloc, wide, step),
-        out_shape=[jax.ShapeDtypeStruct((2,) + padded, f32)]
+        out_shape=[jax.ShapeDtypeStruct((LEAD, LANES), f32)]
         + [jax.ShapeDtypeStruct((2 * mloc * wide, LANES), bf16)] * half,
         in_specs=[VMEM] * 2,
         out_specs=[VMEM] * (half + 1),
+        scratch_shapes=[pltpu.VMEM((2, 1) + padded[1:], f32)],
         compiler_params=PARAMS,
         name="edges",
-    )(swap(view), ours)
+    )(theirs, ours)
     raws = [permute(sends[q - 1], members, tiles, lambda m, t: (m ^ (2 * q + 1), t)) for q in range(1, half)]
-    *raws, both = lax.optimization_barrier((*raws, both))
+    *raws, rim = lax.optimization_barrier((*raws, rim))
     block = pl.pallas_call(
         functools.partial(block_kernel, mloc, width, step),
         out_shape=jax.ShapeDtypeStruct((planes, 2 * mloc * width, LANES), bf16),
-        in_specs=[VMEM],
+        in_specs=[VMEM] * 3,
         out_specs=VMEM,
+        scratch_shapes=[pltpu.VMEM((2,) + padded, f32)],
         compiler_params=PARAMS,
         name="block",
-    )(both)
+    )(theirs, ours, rim)
     kept = jax.ShapeDtypeStruct((half - 1, planes * width, LANES), bf16)
     crossed = pl.pallas_call(
         functools.partial(cross_kernel, mloc, width, wide, step),

time: 10.8 us -> 10.8 us (level)
  transfers between devices with their start and end apart: 7 -> 7, of which waited for: 4 -> 4; matrix products, arithmetic and copies ran while one was open for 0% -> 0% of each run, Pallas kernels for 14% -> 15%
where the time goes in v7:
time: 10.8 us; the launch traced here: 10.6 us
  starting transfers between devices  5.96 us (55%)
  Pallas kernels  2.46 us (23%)
  waiting for transfers between devices  1.7 us (16%)
  local copies, waits for them, and re-layouts  0.45 us (4%)
    ppermute x7, starting transfers between devices, permute(): return lax.ppermute(value, ('member', 'tile'), pairs)  5.96 us
    pallas_call x2, Pallas kernels, local(): pl.pallas_call(functools.partial(half_kernel, wide, step, total, 2 * mloc...  1.79 us
    ppermute x7, waiting for transfers between devices, permute(): return lax.ppermute(value, ('member', 'tile'), pairs)  1.7 us
    pallas_call x1, Pallas kernels, local(): pl.pallas_call(functools.partial(inner_kernel, mloc, width, step, total),...  0.54 us
    unnamed x2, local copies, waits for them, and re-layouts  0.45 us
  transfers between devices with their start and end apart: 7, of which 4 were waited for; matrix products, arithmetic and copies ran while one was open for 0% of the time, Pallas kernels for 15%

profile of v7, /device:TPU:0, one launch (start us, length us, event | category | flops | bytes accessed | tf_op | source)
XLA Modules:
  0.0 10.6 jit_solution(11070049791021724953)
XLA Ops:
  0.0 0.0 copy-start
  0.0 0.5 %collective-permute-start = (f32[6,48,128]{2,1,0:T(8,128)}, f32[6,48,128]{2,1,0:T(8,128)S(1)}, u32[]{:S(2)}, u32[]{:S(2)}) collective-permute-start(f32[6,48,128]{2,1,0:T(8,128)} %bitcast.6), channel_id=1, source_target_pairs={{0,8},{1,9},{2,10},{3,11},{4,12},{5,13},{6,14},{7,15},{8,0},{9,1},... | collective-permute-start | bytes 442376 | tf_op jit(solution)/shard_map/ppermute | solution.py:27
  0.5 0.5 %copy-done = f32[2,6,3072]{2,0,1:T(2,128)S(1)} copy-done((f32[2,6,3072]{2,0,1:T(2,128)S(1)}, f32[2,6,3072]{2,0,1:T(2,128)}, u32[]{:S(2)}) %copy-start) | copy-done | bytes 147480
  0.9 2.4 %collective-permute-start.3 = (bf16[6,32,128]{2,1,0:T(8,128)(2,1)S(1)}, bf16[6,32,128]{2,1,0:T(8,128)(2,1)S(1)}, u32[]{:S(2)}, u32[]{:S(2)}) collective-permute-start(bf16[6,32,128]{2,1,0:T(8,128)(2,1)S(1)} %get-tuple-element.24), channel_id=1, source_target_pairs={{0,24},{1,25},{2,26},{3,27},{4,28},{5,29},{6,30},{7,31},{8,16},{9,... | collective-permute-start | bytes 147464 | tf_op jit(solution)/shard_map/ppermute | solution.py:27
  3.4 0.0 collective-permute-done.theirs
  3.4 1.2 %collective-permute-start.1 = (bf16[64,128]{1,0:T(8,128)(2,1)S(1)}, bf16[64,128]{1,0:T(8,128)(2,1)S(1)}, u32[]{:S(2)}, u32[]{:S(2)}) collective-permute-start(bf16[64,128]{1,0:T(8,128)(2,1)S(1)} %get-tuple-element.22), channel_id=1, source_target_pairs={{0,16},{1,24},{2,19},{3,18},{4,21},{5,20},{6,31},{7,23},{8,17},{9,... | collective-permute-start | bytes 49160 | tf_op jit(solution)/shard_map/ppermute | solution.py:27
  4.6 1.2 %collective-permute-start.2 = (bf16[64,128]{1,0:T(8,128)(2,1)S(1)}, bf16[64,128]{1,0:T(8,128)(2,1)S(1)}, u32[]{:S(2)}, u32[]{:S(2)}) collective-permute-start(bf16[64,128]{1,0:T(8,128)(2,1)S(1)} %get-tuple-element.23), channel_id=1, source_target_pairs={{0,1},{1,0},{2,3},{3,2},{4,5},{5,4},{6,7},{7,6},{8,24},{9,10},{10,... | collective-permute-start | bytes 49160 | tf_op jit(solution)/shard_map/ppermute | solution.py:27
  5.8 0.0 collective-permute-done.3.refs_0_
  5.9 0.5 %collective-permute-start.4 = (bf16[1,60,128]{2,1,0:T(8,128)(2,1)S(1)}, bf16[1,60,128]{2,1,0:T(8,128)(2,1)S(1)}, u32[]{:S(2)}, u32[]{:S(2)}) collective-permute-start(bf16[1,60,128]{2,1,0:T(8,128)(2,1)S(1)} %get-tuple-element.30), channel_id=1, source_target_pairs={{0,8},{1,9},{2,10},{3,11},{4,12},{5,13},{6,14},{7,15},{8,0},{9,1},... | collective-permute-start | bytes 46088 | tf_op jit(solution)/shard_map/ppermute | solution.py:27
  6.4 0.1 collective-permute-start.5
  6.5 0.1 block.1
  6.5 0.7 %collective-permute-done.4.refs_2_ = bf16[1,60,128]{2,1,0:T(8,128)(2,1)S(1)} collective-permute-done((bf16[1,60,128]{2,1,0:T(8,128)(2,1)S(1)}, bf16[1,60,128]{2,1,0:T(8,128)(2,1)S(1)}, u32[]{:S(2)}, u32[]{:S(2)}) %collective-permute-start.4) | collective-permute-done | bytes 15392 | tf_op jit(solution)/shard_map/ppermute | solution.py:27
  7.2 0.3 %collective-permute-done.5.refs_3_ = bf16[1,60,128]{2,1,0:T(8,128)(2,1)S(1)} collective-permute-done((bf16[1,60,128]{2,1,0:T(8,128)(2,1)S(1)}, bf16[1,60,128]{2,1,0:T(8,128)(2,1)S(1)}, u32[]{:S(2)}, u32[]{:S(2)}) %collective-permute-start.5) | collective-permute-done | bytes 15392 | tf_op jit(solution)/shard_map/ppermute | solution.py:27
  7.6 0.5 %inner.1 = (f32[4,26,768]{2,1,0:T(8,128)S(1)}, f32[1,4,6,8,128]{4,3,2,1,0:T(8,128)S(1)}) custom-call(bf16[6,40,128]{2,1,0:T(8,128)(2,1)S(1)} %block.1, bf16[1,60,128]{2,1,0:T(8,128)(2,1)S(1)} %get-tuple-element.28.refs_0_, bf16[1,60,128]{2,1,0:T(8,128)(2,1)S(1)} %get-tuple-element.29.refs_1_, bf16[1,60,128]{2,1,0:T(8,128)(2,1)S(1)} %collective-permute-done.4.refs_2_, ...), custom_call_target="tpu_custom_call" | custom-call | tf_op jit(solution)/shard_map/inner/pallas_call | solution.py:322
  8.1 0.0 collective-permute-done.1.refs_0_
  8.1 0.4 %collective-permute-done.2.refs_1_ = bf16[64,128]{1,0:T(8,128)(2,1)S(1)} collective-permute-done((bf16[64,128]{1,0:T(8,128)(2,1)S(1)}, bf16[64,128]{1,0:T(8,128)(2,1)S(1)}, u32[]{:S(2)}, u32[]{:S(2)}) %collective-permute-start.2) | collective-permute-done | bytes 16416 | tf_op jit(solution)/shard_map/ppermute | solution.py:27
  8.5 0.0 collective-permute-start.6
  8.6 0.9 %outer.2.refs_3_ = f32[6,26,768]{2,1,0:T(8,128)} custom-call(bf16[128,128]{1,0:T(8,128)(2,1)S(1)} %join.1.refs_0_, f32[1,4,6,8,128]{4,3,2,1,0:T(8,128)S(1)} %get-tuple-element.35.refs_1_.refs_2_, f32[4,26,768]{2,1,0:T(8,128)S(1)} %get-tuple-element.36.refs_2_), custom_call_target="tpu_custom_call" | custom-call | tf_op jit(solution)/shard_map/outer/pallas_call | solution.py:345
  9.5 0.3 %collective-permute-done.6.refs_1_ = bf16[128,128]{1,0:T(8,128)(2,1)S(1)} collective-permute-done((bf16[128,128]{1,0:T(8,128)(2,1)S(1)}, bf16[128,128]{1,0:T(8,128)(2,1)S(1)}, u32[]{:S(2)}, u32[]{:S(2)}) %collective-permute-start.6) | collective-permute-done | bytes 32800 | tf_op jit(solution)/shard_map/ppermute | solution.py:27
  9.7 0.9 %outer.3 = f32[6,26,768]{2,1,0:T(8,128)} custom-call(bf16[128,128]{1,0:T(8,128)(2,1)S(1)} %join.1.refs_0_, bf16[128,128]{1,0:T(8,128)(2,1)S(1)} %collective-permute-done.6.refs_1_, f32[1,4,6,8,128]{4,3,2,1,0:T(8,128)S(1)} %get-tuple-element.35.refs_1_.refs_2_, f32[6,26,768]{2,1,0:T(8,128)} %outer.2.refs_3_), custom_call_target="tpu_custom_call", output_to_operand_aliasing={{}: (3, {})} | custom-call | tf_op jit(solution)/shard_map/outer/pallas_call | solution.py:345
  (5 shorter events, 0.1 us)
Async XLA Ops:
  0.0 0.9 %copy-start = (f32[2,6,3072]{2,0,1:T(2,128)S(1)}, f32[2,6,3072]{2,0,1:T(2,128)}, u32[]{:S(2)}) copy-start(f32[2,6,3072]{2,0,1:T(2,128)} %param.1) | copy-start | bytes 442372
  0.0 3.4 %collective-permute-start = (f32[6,48,128]{2,1,0:T(8,128)}, f32[6,48,128]{2,1,0:T(8,128)S(1)}, u32[]{:S(2)}, u32[]{:S(2)}) collective-permute-start(f32[6,48,128]{2,1,0:T(8,128)} %bitcast.6), channel_id=1, source_target_pairs={{0,8},{1,9},{2,10},{3,11},{4,12},{5,13},{6,14},{7,15},{8,0},{9,1},... | collective-permute-start | bytes 442376 | tf_op jit(solution)/shard_map/ppermute | solution.py:27
  0.9 4.9 %collective-permute-start.3 = (bf16[6,32,128]{2,1,0:T(8,128)(2,1)S(1)}, bf16[6,32,128]{2,1,0:T(8,128)(2,1)S(1)}, u32[]{:S(2)}, u32[]{:S(2)}) collective-permute-start(bf16[6,32,128]{2,1,0:T(8,128)(2,1)S(1)} %get-tuple-element.24), channel_id=1, source_target_pairs={{0,24},{1,25},{2,26},{3,27},{4,28},{5,29},{6,30},{7,31},{8,16},{9,... | collective-permute-start | bytes 147464 | tf_op jit(solution)/shard_map/ppermute | solution.py:27
  3.4 4.7 %collective-permute-start.1 = (bf16[64,128]{1,0:T(8,128)(2,1)S(1)}, bf16[64,128]{1,0:T(8,128)(2,1)S(1)}, u32[]{:S(2)}, u32[]{:S(2)}) collective-permute-start(bf16[64,128]{1,0:T(8,128)(2,1)S(1)} %get-tuple-element.22), channel_id=1, source_target_pairs={{0,16},{1,24},{2,19},{3,18},{4,21},{5,20},{6,31},{7,23},{8,17},{9,... | collective-permute-start | bytes 49160 | tf_op jit(solution)/shard_map/ppermute | solution.py:27
  4.6 3.9 %collective-permute-start.2 = (bf16[64,128]{1,0:T(8,128)(2,1)S(1)}, bf16[64,128]{1,0:T(8,128)(2,1)S(1)}, u32[]{:S(2)}, u32[]{:S(2)}) collective-permute-start(bf16[64,128]{1,0:T(8,128)(2,1)S(1)} %get-tuple-element.23), channel_id=1, source_target_pairs={{0,1},{1,0},{2,3},{3,2},{4,5},{5,4},{6,7},{7,6},{8,24},{9,10},{10,... | collective-permute-start | bytes 49160 | tf_op jit(solution)/shard_map/ppermute | solution.py:27
  5.9 1.4 %collective-permute-start.4 = (bf16[1,60,128]{2,1,0:T(8,128)(2,1)S(1)}, bf16[1,60,128]{2,1,0:T(8,128)(2,1)S(1)}, u32[]{:S(2)}, u32[]{:S(2)}) collective-permute-start(bf16[1,60,128]{2,1,0:T(8,128)(2,1)S(1)} %get-tuple-element.30), channel_id=1, source_target_pairs={{0,8},{1,9},{2,10},{3,11},{4,12},{5,13},{6,14},{7,15},{8,0},{9,1},... | collective-permute-start | bytes 46088 | tf_op jit(solution)/shard_map/ppermute | solution.py:27
  6.4 1.2 %collective-permute-start.5 = (bf16[1,60,128]{2,1,0:T(8,128)(2,1)S(1)}, bf16[1,60,128]{2,1,0:T(8,128)(2,1)S(1)}, u32[]{:S(2)}, u32[]{:S(2)}) collective-permute-start(bf16[1,60,128]{2,1,0:T(8,128)(2,1)S(1)} %get-tuple-element.31), channel_id=1, source_target_pairs={{0,8},{1,9},{2,10},{3,11},{4,12},{5,13},{6,14},{7,15},{8,0},{9,1},... | collective-permute-start | bytes 46088 | tf_op jit(solution)/shard_map/ppermute | solution.py:27
  8.5 1.2 %collective-permute-start.6 = (bf16[128,128]{1,0:T(8,128)(2,1)S(1)}, bf16[128,128]{1,0:T(8,128)(2,1)S(1)}, u32[]{:S(2)}, u32[]{:S(2)}) collective-permute-start(bf16[128,128]{1,0:T(8,128)(2,1)S(1)} %join.1.refs_0_), channel_id=1, source_target_pairs={{0,8},{1,9},{2,10},{3,11},{4,12},{5,13},{6,14},{7,15},{8,0},{9,1},... | collective-permute-start | bytes 98312 | tf_op jit(solution)/shard_map/ppermute | solution.py:27

commit v8 on v7

--- a/solution.py
+++ b/solution.py
@@ -328,8 +328,6 @@
         compiler_params=PARAMS,
         name="inner",
     )(block, *keeps, *cames)
-    *got, part = lax.optimization_barrier((*got[::-1], part))
-    got = got[::-1]
     got = pl.pallas_call(
         join_kernel,
         out_shape=jax.ShapeDtypeStruct((total * wide, LANES), bf16),

time: 10.8 us -> 12.9 us (1.19)
  waiting for transfers between devices: 1.7 us -> 3.74 us
    ppermute x7, waiting for transfers between devices: 1.7 us -> 3.74 us  [permute(): return lax.ppermute(value, ('member', 'tile'), pairs)]
  transfers between devices with their start and end apart: 7 -> 7, of which waited for: 4 -> 4; matrix products, arithmetic and copies ran while one was open for 0% -> 0% of each run, Pallas kernels for 15% -> 12%
where the time goes in v8:
time: 12.9 us; the launch traced here: 12.7 us
  starting transfers between devices  5.96 us (46%)
  waiting for transfers between devices  3.74 us (29%)
  Pallas kernels  2.49 us (19%)
  local copies, waits for them, and re-layouts  0.45 us (3%)
    ppermute x7, starting transfers between devices, permute(): return lax.ppermute(value, ('member', 'tile'), pairs)  5.96 us
    ppermute x7, waiting for transfers between devices, permute(): return lax.ppermute(value, ('member', 'tile'), pairs)  3.74 us
    pallas_call x2, Pallas kernels, local(): pl.pallas_call(functools.partial(half_kernel, wide, step, total, 2 * mloc...  1.82 us
    pallas_call x1, Pallas kernels, local(): pl.pallas_call(functools.partial(inner_kernel, mloc, width, step, total),...  0.54 us
    unnamed x2, local copies, waits for them, and re-layouts  0.45 us
  transfers between devices with their start and end apart: 7, of which 4 were waited for; matrix products, arithmetic and copies ran while one was open for 0% of the time, Pallas kernels for 12%

profile of v8, /device:TPU:0, one launch (start us, length us, event | category | flops | bytes accessed | tf_op | source)
XLA Modules:
  0.0 12.7 jit_solution(15726792336000214475)
XLA Ops:
  0.0 0.0 copy-start
  0.0 0.5 %collective-permute-start = (f32[6,48,128]{2,1,0:T(8,128)}, f32[6,48,128]{2,1,0:T(8,128)S(1)}, u32[]{:S(2)}, u32[]{:S(2)}) collective-permute-start(f32[6,48,128]{2,1,0:T(8,128)} %bitcast.6), channel_id=1, source_target_pairs={{0,8},{1,9},{2,10},{3,11},{4,12},{5,13},{6,14},{7,15},{8,0},{9,1},... | collective-permute-start | bytes 442376 | tf_op jit(solution)/shard_map/ppermute | solution.py:27
  0.5 0.5 %copy-done = f32[2,6,3072]{2,0,1:T(2,128)S(1)} copy-done((f32[2,6,3072]{2,0,1:T(2,128)S(1)}, f32[2,6,3072]{2,0,1:T(2,128)}, u32[]{:S(2)}) %copy-start) | copy-done | bytes 147480
  0.9 2.4 %collective-permute-start.4 = (bf16[6,32,128]{2,1,0:T(8,128)(2,1)S(1)}, bf16[6,32,128]{2,1,0:T(8,128)(2,1)S(1)}, u32[]{:S(2)}, u32[]{:S(2)}) collective-permute-start(bf16[6,32,128]{2,1,0:T(8,128)(2,1)S(1)} %get-tuple-element.21), channel_id=1, source_target_pairs={{0,24},{1,25},{2,26},{3,27},{4,28},{5,29},{6,30},{7,31},{8,16},{9,... | collective-permute-start | bytes 147464 | tf_op jit(solution)/shard_map/ppermute | solution.py:27
  3.4 0.0 collective-permute-done.theirs
  3.4 1.2 %collective-permute-start.1 = (bf16[64,128]{1,0:T(8,128)(2,1)S(1)}, bf16[64,128]{1,0:T(8,128)(2,1)S(1)}, u32[]{:S(2)}, u32[]{:S(2)}) collective-permute-start(bf16[64,128]{1,0:T(8,128)(2,1)S(1)} %get-tuple-element.19), channel_id=1, source_target_pairs={{0,16},{1,24},{2,19},{3,18},{4,21},{5,20},{6,31},{7,23},{8,17},{9,... | collective-permute-start | bytes 49160 | tf_op jit(solution)/shard_map/ppermute | solution.py:27
  4.6 1.2 %collective-permute-start.2 = (bf16[64,128]{1,0:T(8,128)(2,1)S(1)}, bf16[64,128]{1,0:T(8,128)(2,1)S(1)}, u32[]{:S(2)}, u32[]{:S(2)}) collective-permute-start(bf16[64,128]{1,0:T(8,128)(2,1)S(1)} %get-tuple-element.20), channel_id=1, source_target_pairs={{0,1},{1,0},{2,3},{3,2},{4,5},{5,4},{6,7},{7,6},{8,24},{9,10},{10,... | collective-permute-start | bytes 49160 | tf_op jit(solution)/shard_map/ppermute | solution.py:27
  5.8 1.4 %collective-permute-done.1.refs_0_ = bf16[64,128]{1,0:T(8,128)(2,1)S(1)} collective-permute-done((bf16[64,128]{1,0:T(8,128)(2,1)S(1)}, bf16[64,128]{1,0:T(8,128)(2,1)S(1)}, u32[]{:S(2)}, u32[]{:S(2)}) %collective-permute-start.1) | collective-permute-done | bytes 16416 | tf_op jit(solution)/shard_map/ppermute | solution.py:27
  7.2 1.3 %collective-permute-done.2.refs_1_ = bf16[64,128]{1,0:T(8,128)(2,1)S(1)} collective-permute-done((bf16[64,128]{1,0:T(8,128)(2,1)S(1)}, bf16[64,128]{1,0:T(8,128)(2,1)S(1)}, u32[]{:S(2)}, u32[]{:S(2)}) %collective-permute-start.2) | collective-permute-done | bytes 16416 | tf_op jit(solution)/shard_map/ppermute | solution.py:27
  8.5 0.0 collective-permute-start.3
  8.6 0.0 collective-permute-done.4.refs_0_
  8.6 0.5 %collective-permute-start.5 = (bf16[1,60,128]{2,1,0:T(8,128)(2,1)S(1)}, bf16[1,60,128]{2,1,0:T(8,128)(2,1)S(1)}, u32[]{:S(2)}, u32[]{:S(2)}) collective-permute-start(bf16[1,60,128]{2,1,0:T(8,128)(2,1)S(1)} %get-tuple-element.27), channel_id=1, source_target_pairs={{0,8},{1,9},{2,10},{3,11},{4,12},{5,13},{6,14},{7,15},{8,0},{9,1},... | collective-permute-start | bytes 46088 | tf_op jit(solution)/shard_map/ppermute | solution.py:27
  9.1 0.1 collective-permute-start.6
  9.2 0.1 block.1
  9.3 0.7 %collective-permute-done.5.refs_2_ = bf16[1,60,128]{2,1,0:T(8,128)(2,1)S(1)} collective-permute-done((bf16[1,60,128]{2,1,0:T(8,128)(2,1)S(1)}, bf16[1,60,128]{2,1,0:T(8,128)(2,1)S(1)}, u32[]{:S(2)}, u32[]{:S(2)}) %collective-permute-start.5) | collective-permute-done | bytes 15392 | tf_op jit(solution)/shard_map/ppermute | solution.py:27
  10.0 0.3 %collective-permute-done.6.refs_3_ = bf16[1,60,128]{2,1,0:T(8,128)(2,1)S(1)} collective-permute-done((bf16[1,60,128]{2,1,0:T(8,128)(2,1)S(1)}, bf16[1,60,128]{2,1,0:T(8,128)(2,1)S(1)}, u32[]{:S(2)}, u32[]{:S(2)}) %collective-permute-start.6) | collective-permute-done | bytes 15392 | tf_op jit(solution)/shard_map/ppermute | solution.py:27
  10.3 0.5 %inner.1 = (f32[4,26,768]{2,1,0:T(8,128)S(1)}, f32[1,4,6,8,128]{4,3,2,1,0:T(8,128)S(1)}) custom-call(bf16[6,40,128]{2,1,0:T(8,128)(2,1)S(1)} %block.1, bf16[1,60,128]{2,1,0:T(8,128)(2,1)S(1)} %get-tuple-element.25.refs_0_, bf16[1,60,128]{2,1,0:T(8,128)(2,1)S(1)} %get-tuple-element.26.refs_1_, bf16[1,60,128]{2,1,0:T(8,128)(2,1)S(1)} %collective-permute-done.5.refs_2_, ...), custom_call_target="tpu_custom_call" | custom-call | tf_op jit(solution)/shard_map/inner/pallas_call | solution.py:322
  10.9 0.9 %outer.2.refs_3_ = f32[6,26,768]{2,1,0:T(8,128)} custom-call(bf16[128,128]{1,0:T(8,128)(2,1)S(1)} %join.1.refs_0_, f32[1,4,6,8,128]{4,3,2,1,0:T(8,128)S(1)} %get-tuple-element.29.refs_1_.refs_2_, f32[4,26,768]{2,1,0:T(8,128)S(1)} %get-tuple-element.30.refs_2_), custom_call_target="tpu_custom_call" | custom-call | tf_op jit(solution)/shard_map/outer/pallas_call | solution.py:343
  11.8 0.0 collective-permute-done.3.refs_1_
  11.8 0.9 %outer.3 = f32[6,26,768]{2,1,0:T(8,128)} custom-call(bf16[128,128]{1,0:T(8,128)(2,1)S(1)} %join.1.refs_0_, bf16[128,128]{1,0:T(8,128)(2,1)S(1)} %collective-permute-done.3.refs_1_, f32[1,4,6,8,128]{4,3,2,1,0:T(8,128)S(1)} %get-tuple-element.29.refs_1_.refs_2_, f32[6,26,768]{2,1,0:T(8,128)} %outer.2.refs_3_), custom_call_target="tpu_custom_call", output_to_operand_aliasing={{}: (3, {})} | custom-call | tf_op jit(solution)/shard_map/outer/pallas_call | solution.py:343
  (5 shorter events, 0.1 us)
Async XLA Ops:
  0.0 0.9 %copy-start = (f32[2,6,3072]{2,0,1:T(2,128)S(1)}, f32[2,6,3072]{2,0,1:T(2,128)}, u32[]{:S(2)}) copy-start(f32[2,6,3072]{2,0,1:T(2,128)} %param.1) | copy-start | bytes 442372
  0.0 3.4 %collective-permute-start = (f32[6,48,128]{2,1,0:T(8,128)}, f32[6,48,128]{2,1,0:T(8,128)S(1)}, u32[]{:S(2)}, u32[]{:S(2)}) collective-permute-start(f32[6,48,128]{2,1,0:T(8,128)} %bitcast.6), channel_id=1, source_target_pairs={{0,8},{1,9},{2,10},{3,11},{4,12},{5,13},{6,14},{7,15},{8,0},{9,1},... | collective-permute-start | bytes 442376 | tf_op jit(solution)/shard_map/ppermute | solution.py:27
  0.9 7.6 %collective-permute-start.4 = (bf16[6,32,128]{2,1,0:T(8,128)(2,1)S(1)}, bf16[6,32,128]{2,1,0:T(8,128)(2,1)S(1)}, u32[]{:S(2)}, u32[]{:S(2)}) collective-permute-start(bf16[6,32,128]{2,1,0:T(8,128)(2,1)S(1)} %get-tuple-element.21), channel_id=1, source_target_pairs={{0,24},{1,25},{2,26},{3,27},{4,28},{5,29},{6,30},{7,31},{8,16},{9,... | collective-permute-start | bytes 147464 | tf_op jit(solution)/shard_map/ppermute | solution.py:27
  3.4 3.8 %collective-permute-start.1 = (bf16[64,128]{1,0:T(8,128)(2,1)S(1)}, bf16[64,128]{1,0:T(8,128)(2,1)S(1)}, u32[]{:S(2)}, u32[]{:S(2)}) collective-permute-start(bf16[64,128]{1,0:T(8,128)(2,1)S(1)} %get-tuple-element.19), channel_id=1, source_target_pairs={{0,16},{1,24},{2,19},{3,18},{4,21},{5,20},{6,31},{7,23},{8,17},{9,... | collective-permute-start | bytes 49160 | tf_op jit(solution)/shard_map/ppermute | solution.py:27
  4.6 3.9 %collective-permute-start.2 = (bf16[64,128]{1,0:T(8,128)(2,1)S(1)}, bf16[64,128]{1,0:T(8,128)(2,1)S(1)}, u32[]{:S(2)}, u32[]{:S(2)}) collective-permute-start(bf16[64,128]{1,0:T(8,128)(2,1)S(1)} %get-tuple-element.20), channel_id=1, source_target_pairs={{0,1},{1,0},{2,3},{3,2},{4,5},{5,4},{6,7},{7,6},{8,24},{9,10},{10,... | collective-permute-start | bytes 49160 | tf_op jit(solution)/shard_map/ppermute | solution.py:27
  8.5 3.3 %collective-permute-start.3 = (bf16[128,128]{1,0:T(8,128)(2,1)S(1)}, bf16[128,128]{1,0:T(8,128)(2,1)S(1)}, u32[]{:S(2)}, u32[]{:S(2)}) collective-permute-start(bf16[128,128]{1,0:T(8,128)(2,1)S(1)} %join.1.refs_0_), channel_id=1, source_target_pairs={{0,8},{1,9},{2,10},{3,11},{4,12},{5,13},{6,14},{7,15},{8,0},{9,1},... | collective-permute-start | bytes 98312 | tf_op jit(solution)/shard_map/ppermute | solution.py:27
  8.6 1.4 %collective-permute-start.5 = (bf16[1,60,128]{2,1,0:T(8,128)(2,1)S(1)}, bf16[1,60,128]{2,1,0:T(8,128)(2,1)S(1)}, u32[]{:S(2)}, u32[]{:S(2)}) collective-permute-start(bf16[1,60,128]{2,1,0:T(8,128)(2,1)S(1)} %get-tuple-element.27), channel_id=1, source_target_pairs={{0,8},{1,9},{2,10},{3,11},{4,12},{5,13},{6,14},{7,15},{8,0},{9,1},... | collective-permute-start | bytes 46088 | tf_op jit(solution)/shard_map/ppermute | solution.py:27
  9.1 1.2 %collective-permute-start.6 = (bf16[1,60,128]{2,1,0:T(8,128)(2,1)S(1)}, bf16[1,60,128]{2,1,0:T(8,128)(2,1)S(1)}, u32[]{:S(2)}, u32[]{:S(2)}) collective-permute-start(bf16[1,60,128]{2,1,0:T(8,128)(2,1)S(1)} %get-tuple-element.28), channel_id=1, source_target_pairs={{0,8},{1,9},{2,10},{3,11},{4,12},{5,13},{6,14},{7,15},{8,0},{9,1},... | collective-permute-start | bytes 46088 | tf_op jit(solution)/shard_map/ppermute | solution.py:27
